TPU v7x, 32 devices: a whole 2x2x4 slice. The times are simulated.
32 devices in a mesh: head: 4 (over x, core), blk: 8 (over z, y).
Axes of the slice: x: 2, y: 2, z: 4, core: 2. Of those that a mesh axis runs over, the one named last changes fastest.
Arguments:
- tokens: bfloat16 [16384, 768], P(('blk', 'head')), may hold values from -6 to 6
- first_values: bfloat16 [16384, 384], P(('blk', 'head')), may hold values from -6 to 6
- cotangent: bfloat16 [16384, 768], P(('blk', 'head')), may hold values from -6 to 6
- w_query: bfloat16 [768, 768], P('blk', 'head'), may hold values from -0.21875 to 0.21875
- w_key: bfloat16 [768, 768], P('blk', 'head'), may hold values from -0.21875 to 0.21875
- w_value: bfloat16 [768, 384], P('blk', 'head'), may hold values from -0.21875 to 0.21875
- w_out: bfloat16 [768, 768], P('head', 'blk'), may hold values from -3.5 to 3.5
- w_up: bfloat16 [768, 3072], P('blk', 'head'), may hold values from -0.21875 to 0.21875
- w_down: bfloat16 [3072, 768], P('head', 'blk'), may hold values from -0.109375 to 0.109375
- gain_attn: float32 [768], P('blk'), may hold values from 0.5 to 1.5
- gain_mlp: float32 [768], P('blk'), may hold values from 0.5 to 1.5
- doc_lengths: int32 [16], replicated, may hold values from 1 to 4096, 16384 in all
Outputs:
- layer_output: bfloat16 [16384, 768], P(('blk', 'head'))
- grad_tokens: float32 [16384, 768], P(('blk', 'head'))
- grad_first_values: float32 [16384, 384], P(('blk', 'head'))
- grad_w_query: float32 [768, 768], P('blk', 'head')
- grad_w_key: float32 [768, 768], P('blk', 'head')
- grad_w_value: float32 [768, 384], P('blk', 'head')
- grad_w_out: float32 [768, 768], P('head', 'blk')
- grad_w_up: float32 [768, 3072], P('blk', 'head')
- grad_w_down: float32 [3072, 768], P('head', 'blk')
- grad_gain_attn: float32 [768], P('blk')
- grad_gain_mlp: float32 [768], P('blk')
Inputs may be any that keep to these rules, and one draw needn't show every extreme that they name: `doc_lengths`: the lengths sum to 16384 and the longest is exactly 4096.
All inputs are finite; a program needn't handle non-finite values.
Results may differ from a plain program's by a relative error of at most 0.03.
Values may be sent and summed in bfloat16 or wider, within the bound.
A program may use at most 192 MiB of HBM per device.

v0:
```python
import functools

import jax
import jax.numpy as jnp
from jax import lax
from jax.experimental import pallas as pl
from jax.experimental.pallas import tpu as pltpu
from jax.sharding import PartitionSpec as P

HEADS = 12
HEAD_DIM = 64
DOC_MAX = 4096
EPSILON = 1e-05
GELU_SCALE = 0.7978845608028654
EXCLUDED = -1e30
WIDTH = 256
SPLITS = 3
BF16 = jnp.bfloat16
F32 = jnp.float32
MESH = pl.DeviceIdType.MESH
ANY = pl.BlockSpec(memory_space=pl.ANY)
WHOLE = pl.BlockSpec(memory_space=pltpu.VMEM)
NT = (((1,), (1,)), ((), ()))
TN = (((0,), (0,)), ((), ()))


def dotf(left, right, dims=None):
    if dims is None:
        dims = (((1,), (0,)), ((), ()))
    return lax.dot_general(left, right, dims, preferred_element_type=F32)


def remote(src, dst, send_sem, recv_sem, head, blk):
    return pltpu.make_async_remote_copy(
        src_ref=src,
        dst_ref=dst,
        send_sem=send_sem,
        recv_sem=recv_sem,
        device_id={"head": head, "blk": blk},
        device_id_type=MESH,
    )


def greet(partners):
    barrier = pltpu.get_barrier_semaphore()
    for head, blk in partners:
        pl.semaphore_signal(
            barrier, inc=1, device_id={"head": head, "blk": blk}, device_id_type=MESH
        )
    pl.semaphore_wait(barrier, len(partners))


def xor(value, bit):
    return value + bit - 2 * bit * (lax.div(value, bit) % 2)


def partners_of(head, blk, nblk, heads=True, blks=True):
    found = []
    if heads:
        found += [(xor(head, 1), blk), (xor(head, 2), blk), (3 - head, blk)]
    if blks:
        found += [(head, lax.rem(blk + d, nblk)) for d in range(1, nblk)]
    return found


class Line:
    def __init__(self, nblk, head, blk, source, target, up, down, across):
        self.half, self.head, self.blk = nblk // 2, head, blk
        self.place, self.parity = lax.div(blk, 2), lax.rem(blk, 2)
        self.source, self.target = source, target
        self.sems = {"up": up, "down": down, "across": across}

    def copy(self, way, origin, step, fresh=False):
        slot = 2 * origin + self.parity
        to = {
            "up": lax.rem(self.blk + 2, 2 * self.half),
            "down": lax.rem(self.blk + 2 * self.half - 2, 2 * self.half),
            "across": self.blk + 1 - 2 * self.parity,
        }[way]
        send, recv = self.sems[way]
        return remote(
            self.source if fresh else self.target.at[slot],
            self.target.at[slot], send.at[step], recv.at[step], self.head, to,
        )

    def landing(self, way, slot, step):
        send, recv = self.sems[way]
        other = self.blk + 1 - 2 * self.parity
        at = self.target.at[slot]
        return remote(at, at, send.at[step], recv.at[step], self.head, other)

    def begin(self):
        @pl.when(self.place + 1 < self.half)
        def _():
            self.copy("up", self.place, 0, True).start()

        @pl.when(self.place > 0)
        def _():
            self.copy("down", self.place, 0, True).start()

        self.copy("across", self.place, self.place, True).start()

    def step(self, s, then=None):
        low, high = self.place - 1 - s, self.place + 1 + s

        @pl.when(low >= 0)
        def _():
            self.landing("up", 2 * low + self.parity, s).wait_recv()
            if s + 1 < self.half - 1:

                @pl.when(self.place + 1 < self.half)
                def _():
                    self.copy("up", low, s + 1).start()

            self.copy("across", low, low).start()
            if then:
                then(2 * low + self.parity)

        @pl.when(high < self.half)
        def _():
            self.landing("down", 2 * high + self.parity, s).wait_recv()
            if s + 1 < self.half - 1:

                @pl.when(self.place > 0)
                def _():
                    self.copy("down", high, s + 1).start()

            self.copy("across", high, high).start()
            if then:
                then(2 * high + self.parity)

    def land(self, origin):
        self.landing("across", 2 * origin + 1 - self.parity, origin).wait_recv()

    def finish(self):
        for o in range(self.half):
            self.copy("across", o, o).wait_send()
        for s in range(self.half - 1):

            @pl.when((self.place - s >= 0) & (self.place + 1 < self.half))
            def _():
                self.copy("up", self.place - s, s).wait_send()

            @pl.when((self.place + s < self.half) & (self.place > 0))
            def _():
                self.copy("down", self.place + s, s).wait_send()


def tail_kernel(
    nblk, pieces, cols, d_q, d_k, d_v, normed, w_qk, w_v, gain_m, kept, got, tok, resid, gain,
    out_grad, out_q, out_k, out_v, out_first, out_gain, out_up, out_down, out_out,
    grad, weights, gains, joined, weight, acc, first_got, rest_sum,
    core_buf, side_out, side_buf, pair_buf, line_out, line_in, v_sum, v_got,
    gain_buf, gain_sum, gain_got, up_out, up_in, down_out, down_in,
    own_sem, send_s, recv_s, send_x, recv_x, send_y, recv_y, send_l, recv_l,
    send_v, recv_v, send_f, recv_f, send_g, recv_g, send_h, recv_h, send_u, recv_u, send_d, recv_d,
):
    head, blk = lax.axis_index("head"), lax.axis_index("blk")
    side, core, far = xor(head, 2), xor(head, 1), 3 - head
    greet(partners_of(head, blk, nblk))
    rows = grad.shape[1] // pieces
    line, place, parity = nblk // 2, lax.div(blk, 2), lax.rem(blk, 2)
    pair = blk + 1 - 2 * parity
    above, below = lax.rem(blk + 2, nblk), lax.rem(blk + nblk - 2, nblk)

    def part(ref, p):
        return ref.at[pl.ds(p * rows, rows)]

    def to_core(i, p, slot):
        return remote(
            part(grad.at[slot], p), part(core_buf.at[i], p), send_s.at[i, p], recv_s.at[i, p],
            core, blk,
        )

    def to_side(p):
        return remote(
            part(side_out, p), part(side_buf, p), send_x.at[p], recv_x.at[p], side, blk
        )

    def sum_of(t):
        return kept[t].astype(F32) + got[t].astype(F32)

    def up_copy(t, to):
        return remote(up_out.at[t], up_in.at[t], send_u.at[t], recv_u.at[t], head, to)

    def down_copy(t, to):
        return remote(down_out.at[t], down_in.at[t], send_d.at[t], recv_d.at[t], head, to)

    def first_hops():
        for n in range(line - 1):
            t = line - 1 - n

            @pl.when((place == 0) & (place < t))
            def _():
                up_out[t] = sum_of(t).astype(BF16)
                up_copy(t, above).start()

            @pl.when((place == line - 1) & (place > n))
            def _():
                down_out[n] = sum_of(n).astype(BF16)
                down_copy(n, below).start()

    def next_hops(n):
        t = line - 1 - n

        @pl.when((place > 0) & (place < t))
        def _():
            up_copy(t, above).wait_recv()
            up_out[t] = (sum_of(t) + up_in[t].astype(F32)).astype(BF16)
            up_copy(t, above).start()

        @pl.when((place < line - 1) & (place > n))
        def _():
            down_copy(n, below).wait_recv()
            down_out[n] = (sum_of(n) + down_in[n].astype(F32)).astype(BF16)
            down_copy(n, below).start()

    first_hops()
    half, kind = lax.div(head, 2), lax.rem(head, 2)

    def first_copy(i, to, slot):
        source = d_v.at[pl.ds(to * grad.shape[1], grad.shape[1])]
        return remote(source, first_got.at[slot], send_f.at[i], recv_f.at[slot], to, blk)

    def own_first(slot):
        source = d_v.at[pl.ds(head * grad.shape[1], grad.shape[1])]
        return pltpu.make_async_copy(source, first_got.at[slot], own_sem)

    @pl.when(half == 1)
    def _():
        for i, to in enumerate((core, side, far)):
            first_copy(i, to, kind).start()
        own_first(kind).start()

    mine = half == 0
    weight[:, : 2 * cols] = w_qk[...]
    fresh = jnp.concatenate([w_v[0], w_v[1]], axis=1)
    weight[:, 2 * cols :] = jnp.where(mine, fresh, jnp.zeros_like(fresh))
    gain_row = None
    for i, t in enumerate((far, side, core, head)):
        at = pl.ds(pl.multiple_of(t * grad.shape[1], grad.shape[1]), grad.shape[1])
        joined[:, :cols] = d_q[at, :]
        joined[:, cols : 2 * cols] = d_k[at, :]
        joined[:, 2 * cols : 3 * cols] = d_v[at, :]
        joined[:, 3 * cols :] = jnp.zeros((grad.shape[1], joined.shape[1] - 3 * cols), BF16)
        given = joined[...]
        whole = dotf(given[:, : 3 * cols], weight[...], NT)
        grad[t] = whole.astype(BF16)
        if i == 0:
            for p in range(pieces):
                to_core(0, p, far).start()
        if i == 2:
            for p in range(pieces):
                to_core(1, p, core).start()
        rows_in = normed[at, :]
        term = jnp.sum(whole * rows_in.astype(F32), axis=0, keepdims=True)
        gain_row = term if gain_row is None else gain_row + term
        term = dotf(rows_in, given, TN)
        acc[...] = term if i == 0 else acc[...] + term
        if i == 2:
            for p in range(pieces):
                to_core(0, p, far).wait_recv()
                part(side_out, p)[...] = (
                    part(grad.at[side], p)[...].astype(F32)
                    + part(core_buf.at[0], p)[...].astype(F32)
                ).astype(BF16)
                to_side(p).start()
    whole_part = weights.shape[1]
    for b in range(nblk):
        weights[b] = acc[b * whole_part : (b + 1) * whole_part].astype(BF16)

    def across(n):
        return remote(
            weights.at[2 * n + 1 - parity], pair_buf.at[n], send_y.at[n], recv_y.at[n], head, pair
        )

    for n in range(line):
        across(n).start()
    gain_row = gain_row / gain[...]
    for b in range(nblk):
        gains[b, 0] = gain_row[:, b * whole_part : (b + 1) * whole_part]
        gains[b, 1] = gain_m[:, b * whole_part : (b + 1) * whole_part]

    def gain_to(d):
        to = lax.rem(blk + d, nblk)
        return remote(gains.at[to], gain_buf.at[blk], send_g.at[d], recv_g.at[d], head, to)

    def gain_from(d):
        source = lax.rem(blk - d + nblk, nblk)
        return remote(gains.at[0], gain_buf.at[source], send_g.at[d], recv_g.at[d], head, source)

    for d in range(1, nblk):
        gain_to(d).start()
    gain_buf[blk] = gains[blk]

    def along(d, to):
        return remote(
            line_out.at[to], line_in.at[d], send_l.at[d], recv_l.at[d], head, 2 * to + parity
        )

    next_hops(0)
    for n in range(line):
        across(n).wait_recv()
        line_out[n] = (
            weights[2 * n + parity].astype(F32) + pair_buf[n].astype(F32)
        ).astype(BF16)
    for d in range(1, line):
        along(d, lax.rem(place + d, line)).start()
    for d in range(1, nblk):
        gain_from(d).wait_recv()
    gain_sum[...] = jnp.sum(gain_buf[...], axis=0)
    peers = (core, side, far)

    def gain_copy(i, to):
        return remote(gain_sum, gain_got.at[i], send_h.at[i], recv_h.at[i], to, blk)

    for i, to in enumerate(peers):
        gain_copy(i, to).start()
    for n in range(1, line - 1):
        next_hops(n)
    total = line_out[place].astype(F32)
    for d in range(1, line):
        along(d, lax.rem(place - d + line, line)).wait_recv()
        total = total + line_in[d].astype(F32)
    out_q[...] = total[:, :cols]
    out_k[...] = total[:, cols : 2 * cols]
    v_sum[0] = total[:, 2 * cols : 2 * cols + cols // 2]
    v_sum[1] = total[:, 2 * cols + cols // 2 : 3 * cols]

    def give(c, to):
        return remote(v_sum.at[c], v_got, send_v.at[c], recv_v.at[0], to, blk)

    for c in range(2):
        to = 2 * head + c

        @pl.when((half == 0) & (to != head))
        def _():
            give(c, to).start()

    for p in range(pieces):
        to_core(1, p, core).wait_recv()
        to_side(p).wait_recv()
        norm_grad = (
            part(grad.at[head], p)[...].astype(F32)
            + part(core_buf.at[1], p)[...].astype(F32)
            + part(side_buf, p)[...].astype(F32)
        )
        xhat, scale = statistics(part(tok, p)[...].astype(F32))
        part(out_grad, p)[...] = part(resid, p)[...] + norm_back(norm_grad, xhat, scale, gain[...])
    rest_sum[...] = sum_of(place)
    for t in range(line):

        @pl.when((place == t) & (place > 0))
        def _():
            up_copy(t, above).wait_recv()
            rest_sum[...] += up_in[t].astype(F32)

        @pl.when((place == t) & (place < line - 1))
        def _():
            down_copy(t, below).wait_recv()
            rest_sum[...] += down_in[t].astype(F32)

    inner = out_up.shape[1]
    out_up[...] = rest_sum[:, :inner]
    out_down[...] = rest_sum[:, inner : 2 * inner]
    out_out[...] = rest_sum[:, 2 * inner :].T
    for i, to in enumerate(peers):
        gain_copy(i, to).wait_recv()
    out_gain[...] = gain_sum[...] + gain_got[0] + gain_got[1] + gain_got[2]

    @pl.when(head == 0)
    def _():
        out_v[...] = v_sum[0]

    @pl.when(head != 0)
    def _():
        give(0, half).wait_recv()
        out_v[...] = v_got[...]

    for slot in range(2):

        @pl.when(head == 2 + slot)
        def _():
            own_first(slot).wait()

        @pl.when(head != 2 + slot)
        def _():
            first_copy(0, 2 + slot, slot).wait_recv()

    out_first[...] = jnp.concatenate([first_got[0], first_got[1]], axis=1).astype(F32)

    @pl.when(half == 1)
    def _():
        for i, to in enumerate((core, side, far)):
            first_copy(i, to, kind).wait_send()

    for c in range(2):
        to = 2 * head + c

        @pl.when((half == 0) & (to != head))
        def _():
            give(c, to).wait_send()

    for i, to in enumerate(peers):
        gain_copy(i, to).wait_send()
    for p in range(pieces):
        to_core(0, p, far).wait_send()
        to_core(1, p, core).wait_send()
        to_side(p).wait_send()
    for d in range(1, nblk):
        gain_to(d).wait_send()
    for n in range(line):
        across(n).wait_send()
    for d in range(1, line):
        along(d, lax.rem(place + d, line)).wait_send()
    for t in range(line):

        @pl.when(place < t)
        def _():
            up_copy(t, above).wait_send()

        @pl.when(place > t)
        def _():
            down_copy(t, below).wait_send()


def tail(nblk, d_q, d_k, d_v, normed, w_qk, w_v, gain_m, kept, got, tok, resid, gain, pieces=4):
    dma = pltpu.SemaphoreType.DMA
    row, part, cols = tok.shape, w_v.shape[1] // nblk, d_q.shape[1]
    inner = (kept.shape[2] - cols) // 2
    padded = -(-3 * cols // 128) * 128
    gains = jax.ShapeDtypeStruct((nblk, 2, 1, part), F32)
    half, line = (part, cols // 2), nblk // 2
    piece = (2, pieces)
    vmem = lambda *shape: pltpu.VMEM(shape, BF16)
    return pl.pallas_call(
        functools.partial(tail_kernel, nblk, pieces, cols),
        out_shape=[
            jax.ShapeDtypeStruct(row, F32),
            jax.ShapeDtypeStruct((part, cols), F32),
            jax.ShapeDtypeStruct((part, cols), F32),
            jax.ShapeDtypeStruct(half, F32),
            jax.ShapeDtypeStruct((row[0], 2 * cols), F32),
            jax.ShapeDtypeStruct(gains.shape[1:], F32),
            jax.ShapeDtypeStruct((part, inner), F32),
            jax.ShapeDtypeStruct((part, inner), F32),
            jax.ShapeDtypeStruct((cols, part), F32),
        ],
        in_specs=[WHOLE] * 12,
        out_specs=[WHOLE] * 9,
        scratch_shapes=[
            vmem(4, *row), vmem(nblk, part, padded), pltpu.VMEM(gains.shape, F32),
            vmem(row[0], padded), vmem(row[1], 3 * cols), pltpu.VMEM((row[1], padded), F32),
            vmem(2, row[0], cols), pltpu.VMEM(kept.shape[1:], F32),
            vmem(2, *row), vmem(*row), vmem(*row),
            vmem(line, part, padded), vmem(line, part, padded),
            vmem(line, part, padded),
            pltpu.VMEM((2,) + half, F32),
            pltpu.VMEM(half, F32),
            pltpu.VMEM(gains.shape, F32),
            pltpu.VMEM(gains.shape[1:], F32),
            pltpu.VMEM((3,) + gains.shape[1:], F32),
            vmem(*kept.shape), vmem(*kept.shape), vmem(*kept.shape), vmem(*kept.shape),
            dma,
            dma(piece), dma(piece),
            dma((pieces,)), dma((pieces,)),
            dma((line,)), dma((line,)), dma((line,)), dma((line,)),
            dma((2,)), dma((1,)),
            dma((3,)), dma((2,)),
            dma((nblk,)), dma((nblk,)),
            dma((3,)), dma((3,)),
            dma((line,)), dma((line,)), dma((line,)), dma((line,)),
        ],
        compiler_params=pltpu.CompilerParams(
            collective_id=4, has_side_effects=True, vmem_limit_bytes=60 << 20
        ),
        name="tail",
    )(d_q, d_k, d_v, normed, w_qk, w_v, gain_m, kept, got, tok, resid, gain)


def settle_kernel(count, *refs):
    sources, targets, sems = refs[:count], refs[count : 2 * count], refs[2 * count]
    copies = [
        pltpu.make_async_copy(source, target, sems.at[i])
        for i, (source, target) in enumerate(zip(sources, targets))
    ]
    for copy in copies:
        copy.start()
    for copy in copies:
        copy.wait()


def settle(arrays):
    count = len(arrays)
    return pl.pallas_call(
        functools.partial(settle_kernel, count),
        out_shape=[jax.ShapeDtypeStruct(a.shape, a.dtype) for a in arrays],
        in_specs=[ANY] * count,
        out_specs=[WHOLE] * count,
        scratch_shapes=[pltpu.SemaphoreType.DMA((count,))],
        name="settle",
    )(*arrays)


def statistics(values):
    center = values - jnp.mean(values, axis=-1, keepdims=True)
    scale = lax.rsqrt(jnp.mean(jnp.square(center), axis=-1, keepdims=True) + EPSILON)
    return center * scale, scale


def norm_back(grad, xhat, scale, gain):
    eg = grad * gain
    return scale * (
        eg
        - jnp.mean(eg, axis=-1, keepdims=True)
        - xhat * jnp.mean(eg * xhat, axis=-1, keepdims=True)
    )


def split_parts(values):
    high = values.astype(BF16).astype(F32)
    middle = (values - high).astype(BF16).astype(F32)
    return high, middle, values - high - middle


def front_kernel(
    nblk, parts, pieces, early, tok, first, w_q, w_k, w_v, w_up, w_down, w_out, gain_a, gain_m,
    normed, query, own, near_far, rest, qk_all, v_all, attn_gain, mlp_gain,
    tok_all, first_all, v_own, gain_all, w_qk, w_rest, gains, weight, normed_buf,
    own_sem, normed_sem, send_t, recv_t, send_s, recv_s, send_p, recv_p, send_w, recv_w,
    send_v, recv_v, qk_u, qk_ur, qk_d, qk_dr, qk_a, qk_ar, up_u, up_ur, up_d, up_dr, up_a, up_ar,
    send_x, recv_x, send_c, recv_c, send_f, recv_f, send_z, recv_z, send_y, recv_y,
):
    head, blk = lax.axis_index("head"), lax.axis_index("blk")
    side, core, beyond = xor(head, 2), xor(head, 1), 3 - head
    odd, place = lax.rem(blk, 2), lax.div(blk, 2)
    near = blk + 1 - 2 * odd
    up, down = lax.rem(blk + 2, nblk), lax.rem(blk + nblk - 2, nblk)
    greet(partners_of(head, blk, nblk))
    moved = [(tok, tok_all), (first, first_all)]
    weights = [(w_v, v_own), (gains, gain_all)]
    rows = tok.shape[0] // parts

    def part(ref, n):
        return ref.at[pl.ds(n * rows, rows)]

    def hop(sems, k, n, source, slot, target):
        dst = part(moved[k][1].at[slot], n)
        return remote(source, dst, sems[0].at[k, n], sems[1].at[k, n], target, blk)

    ts, ss, ps = (send_t, recv_t), (send_s, recv_s), (send_p, recv_p)
    order = [(k, n) for n in range(parts) for k in range(2)]
    for k, n in order:
        hop(ts, k, n, part(moved[k][0], n), head, side).start()
    cols, inner = w_q.shape[1], w_up.shape[1]
    w_qk[:, :cols] = w_q[...]
    w_qk[:, cols:] = w_k[...]
    qk_line = Line(nblk, head, blk, w_qk, qk_all, (qk_u, qk_ur), (qk_d, qk_dr), (qk_a, qk_ar))
    qk_line.begin()
    w_rest[:, :inner] = w_up[...]
    w_rest[:, inner : 2 * inner] = w_down[...]
    w_rest[:, 2 * inner :] = w_out[...].T
    line = Line(
        nblk, head, blk, w_rest, rest.at[head], (up_u, up_ur), (up_d, up_dr), (up_a, up_ar)
    )
    line.begin()
    gains[0] = gain_a[...]
    gains[1] = gain_m[...]

    def chunk(sems, slot, b, to, source=None):
        at = rest.at[slot, b]
        return remote(at if source is None else source, at, sems[0].at[b], sems[1].at[b], to, blk)

    xs, cs, fs = (send_x, recv_x), (send_c, recv_c), (send_f, recv_f)

    def to_core(b, source=None):
        chunk(cs, head, b, core, source).start()

    def to_side(b, source=None):
        @pl.when(b < early)
        def _():
            chunk(xs, head, b, side, source).start()

    to_core(blk, w_rest)
    own_rest = pltpu.make_async_copy(w_rest, rest.at[head, blk], own_sem)
    own_rest.start()

    def spread(d):
        to = lax.rem(blk + d, nblk)
        return [
            remote(src, dst.at[blk], send_w.at[i, d], recv_w.at[i, d], head, to)
            for i, (src, dst) in enumerate(weights)
        ]

    def from_peer(d):
        source = lax.rem(blk - d + nblk, nblk)
        return [
            remote(src, dst.at[source], send_w.at[i, d], recv_w.at[i, d], head, source)
            for i, (src, dst) in enumerate(weights)
        ]

    for d in range(1, nblk):
        for copy in spread(d):
            copy.start()
    for k, n in order:
        hop(ss, k, n, part(moved[k][0], n), head, core).start()
    tok_all[head] = tok[...]
    first_all[head] = first[...]
    v_own[blk] = w_v[...]
    gain_all[blk] = gains[...]
    qk_all[blk] = w_qk[...]

    def pass_on(k, n):
        landed = part(moved[k][1].at[side], n)
        hop(ts, k, n, landed, side, side).wait_recv()
        hop(ps, k, n, landed, side, core).start()

    steps = nblk // 2 - 1
    for s in range(steps):
        qk_line.step(s)
    for s in range(steps):
        line.step(s, to_core)
        for k, n in order[s * len(order) // steps : (s + 1) * len(order) // steps]:
            pass_on(k, n)
    to_side(blk, w_rest)
    for s in range(steps):

        @pl.when(place - 1 - s >= 0)
        def _():
            to_side(blk - 2 - 2 * s)

        @pl.when(place + 1 + s < nblk // 2)
        def _():
            to_side(blk + 2 + 2 * s)

    for d in range(1, nblk):
        for copy in from_peer(d):
            copy.wait_recv()
    half, kind = lax.div(head, 2), lax.rem(head, 2)
    for i in range(2):
        target = half + 2 * i

        @pl.when(target == head)
        def _():
            v_all[kind] = v_own[...]

        @pl.when(target != head)
        def _():
            remote(v_own, v_all.at[kind], send_v.at[i], recv_v.at[kind], target, blk).start()

    for o in range(nblk // 2):
        qk_line.land(o)
    for c in range(2):
        source = 2 * kind + c

        @pl.when(source != head)
        def _():
            remote(v_own, v_all.at[c], send_v.at[0], recv_v.at[c], source, blk).wait_recv()

    attn_gain[...] = jnp.concatenate([gain_all[b, 0] for b in range(nblk)], axis=1)
    mlp_gain[...] = jnp.concatenate([gain_all[b, 1] for b in range(nblk)], axis=1)

    step = own.shape[0] // pieces

    def slab(ref, n):
        return ref.at[pl.ds(n * step, step)]

    def far_copy(n, to):
        return remote(slab(own, n), slab(near_far.at[0], n), send_z.at[n], recv_z.at[n], head, to)

    def near_copy(n, src):
        return remote(src, slab(near_far.at[1], n), send_y.at[n], recv_y.at[n], head, near)

    size = HEAD_DIM
    pair = 2 * size
    width = tok.shape[1]
    block = w_q.shape[0]
    for b in range(nblk):
        at = pl.ds(b * block, block)
        both, fresh = qk_all[b], jnp.concatenate([v_all[0, b], v_all[1, b]], axis=1)
        key = both[:, cols:]
        weight[at, :pair] = key[:, :pair]
        weight[at, pair : 2 * pair] = fresh[:, :pair]
        weight[at, 2 * pair : 3 * pair] = jnp.concatenate([key[:, pair:], fresh[:, pair:]], axis=1)
        weight[at, 3 * pair :] = jnp.concatenate(
            [both[:, :cols], jnp.zeros((block, WIDTH - cols), BF16)], axis=1
        )
    stores = []
    for i, t in enumerate((head, side, core, beyond)):
        if i == 2:
            for k, n in order:
                hop(ss, k, n, part(moved[k][1].at[core], n), core, core).wait_recv()
        if i == 3:
            for k, n in order:
                hop(ps, k, n, part(moved[k][1].at[beyond], n), beyond, core).wait_recv()
        total = tok.shape[0]
        at = pl.ds(pl.multiple_of(t * total, total), total)
        xhat, _ = statistics(tok_all[t].astype(F32))
        row = (xhat * attn_gain[...]).astype(BF16)
        normed_buf[t] = row
        stores.append(pltpu.make_async_copy(normed_buf.at[t], normed.at[at], normed_sem.at[i]))
        stores[-1].start()
        out = dotf(row, weight[...])
        query[at, :] = (out[:, 3 * pair :].astype(BF16).astype(F32) * size**-0.5).astype(BF16)
        done = out[:, : 3 * pair].astype(BF16)
        given = first_all[t]
        kept = jnp.where(kind == 0, given[:, :cols], given[:, cols:])
        other = jnp.concatenate(
            [done[:, :pair], kept[:, :pair], done[:, 2 * pair : 2 * pair + size], kept[:, pair:]],
            axis=1,
        )
        own[at, :] = jnp.where(half == 0, done, other)
        for n in range(pieces // 4):
            n = t * (pieces // 4) + n

            @pl.when(blk + 2 < nblk)
            def _():
                far_copy(n, up).start()

            @pl.when(odd == 0)
            def _():
                near_copy(n, slab(own, n)).start()

    for o in range(nblk // 2):

        line.land(o)
        to_core(2 * o + 1 - odd)
        to_side(2 * o + 1 - odd)

    for i, t in enumerate((head, side, core, beyond)):
        for n in range(pieces // 4):
            n = t * (pieces // 4) + n

            @pl.when(blk >= 2)
            def _():
                far_copy(n, down).wait_recv()

            @pl.when((blk >= 2) & (odd == 1))
            def _():
                near_copy(n, slab(near_far.at[0], n)).start()

    own_rest.wait()
    for b in range(early):
        chunk(xs, side, b, side).wait_recv()
        chunk(fs, side, b, core).start()
    for b in range(nblk):
        chunk(cs, core, b, core).wait_recv()
    for b in range(early):
        chunk(fs, beyond, b, core).wait_recv()
        chunk(xs, head, b, side).wait_send()
        chunk(fs, side, b, core).wait_send()
    for b in range(nblk):
        chunk(cs, head, b, core).wait_send()
    for copy in stores:
        copy.wait()
    for n in range(pieces):

        @pl.when((blk >= 2) | (odd == 1))
        def _():
            near_copy(n, slab(own, n)).wait_recv()

        @pl.when(blk + 2 < nblk)
        def _():
            far_copy(n, up).wait_send()

        @pl.when((blk >= 2) | (odd == 0))
        def _():
            near_copy(n, slab(own, n)).wait_send()

    for i in range(2):
        target = half + 2 * i

        @pl.when(target != head)
        def _():
            remote(v_own, v_all.at[kind], send_v.at[i], recv_v.at[kind], target, blk).wait_send()

    for k, n in order:
        hop(ts, k, n, part(moved[k][0], n), head, side).wait_send()
        hop(ss, k, n, part(moved[k][0], n), head, core).wait_send()
        hop(ps, k, n, part(moved[k][1].at[side], n), side, core).wait_send()
    for d in range(1, nblk):
        for copy in spread(d):
            copy.wait_send()
    qk_line.finish()
    line.finish()


def front(
    nblk, early, tok, first, w_q, w_k, w_v, w_up, w_down, w_out, gain_a, gain_m, parts=4, pieces=8
):
    dma = pltpu.SemaphoreType.DMA
    (rows, width), (part, cols) = tok.shape, w_q.shape
    total = 4 * rows
    both = w_up.shape[1] + w_down.shape[1] + w_out.shape[0]
    low = lambda *shape: jax.ShapeDtypeStruct(shape, BF16)
    vmem = lambda *shape: pltpu.VMEM(shape, BF16)
    line = [dma((nblk // 2,))] * 6
    return pl.pallas_call(
        functools.partial(front_kernel, nblk, parts, pieces, early),
        out_shape=[
            low(total, width),
            low(total, WIDTH),
            low(total, 2 * cols),
            low(2, total, 2 * cols),
            low(4, nblk, part, both),
            low(nblk, part, 2 * cols),
            low(2, nblk, *w_v.shape),
            jax.ShapeDtypeStruct((1, width), F32),
            jax.ShapeDtypeStruct((1, width), F32),
        ],
        in_specs=[WHOLE] * 10,
        out_specs=[ANY, WHOLE, WHOLE, ANY, ANY] + [WHOLE] * 4,
        scratch_shapes=[
            vmem(4, *tok.shape),
            vmem(4, *first.shape),
            vmem(nblk, *w_v.shape),
            pltpu.VMEM((nblk, 2) + gain_a.shape, F32),
            vmem(part, 2 * cols),
            vmem(part, both),
            pltpu.VMEM((2,) + gain_a.shape, F32),
            vmem(width, 2 * cols + WIDTH),
            vmem(4, *tok.shape),
            dma,
            dma((4,)),
        ]
        + [dma((2, parts))] * 6
        + [dma((2, nblk))] * 2
        + [dma((2,))] * 2
        + line * 2
        + [dma((nblk,))] * 6
        + [dma((pieces,))] * 4,
        compiler_params=pltpu.CompilerParams(
            collective_id=0, has_side_effects=True, vmem_limit_bytes=56 << 20
        ),
        name="front",
    )(tok, first, w_q, w_k, w_v, w_up, w_down, w_out, gain_a, gain_m)


def gelu_both(pre):
    square = pre * pre
    inner = jnp.tanh(GELU_SCALE * (pre + 0.044715 * square * pre))
    slope = GELU_SCALE * (1.0 + 3.0 * 0.044715 * square)
    outer = 0.5 * (1.0 + inner)
    return pre * outer, outer + 0.5 * pre * (1.0 - inner * inner) * slope


def middle_kernel(
    nblk, up_cols, cross, pieces, tok, mixed_parts, cot, gain, gathered, late, query,
    out, grad_resid, grad_wide, gain_part, keep_up, keep, give, query_later,
    up, down, w_out, up_grad, down_grad, out_grad, mixed, wide_parts, up_got, down_got, out_got,
    sems, out_sems, send_m, recv_m, send_g, recv_g, send_c, recv_c,
    send_z, recv_z, send_y, recv_y, up_side, up_side_got, send_x, recv_x, hidden_all, pre_all, normed_t, cot_t, late_far, send_l, recv_l,
):
    head, blk = lax.axis_index("head"), lax.axis_index("blk")
    x, core_index = lax.div(head, 2), lax.rem(head, 2)
    core = xor(head, 1)
    others = [xor(head, 2), 3 - head, core]
    odd = lax.rem(blk, 2)
    pair = blk + 1 - 2 * odd
    above, below = lax.rem(blk + 2, nblk), lax.rem(blk + nblk - 2, nblk)
    greet(partners_of(head, blk, nblk, blks=False) + [(head, b) for b in (pair, above, below)])
    heads_of = 4
    part = gathered.shape[2]
    cols = mixed.shape[2]
    heads = cols // HEAD_DIM

    def mixed_copy(i, to, slot):
        return remote(
            mixed_parts.at[to], mixed.at[slot], send_m.at[i], recv_m.at[i], to, blk
        )

    for i, to in enumerate(others):
        mixed_copy(i, to, head).start()
    late_copy = remote(late, late_far, send_l, recv_l, core, blk)
    late_copy.start()
    early = nblk - late.shape[0]
    piece_rows = query.shape[0] // pieces

    def slab(ref, p):
        return ref.at[pl.ds(p * piece_rows, piece_rows)]

    def far_copy(p, to):
        dst = slab(query_later.at[1], p)
        return remote(slab(query, p), dst, send_z.at[p], recv_z.at[p], head, to)

    def near_copy(p, src):
        return remote(src, slab(query_later.at[0], p), send_y.at[p], recv_y.at[p], head, pair)

    for p in range(pieces):

        @pl.when(blk >= 2)
        def _():
            far_copy(p, below).start()

        @pl.when(odd == 1)
        def _():
            near_copy(p, slab(query, p)).start()

    def relay(p):
        @pl.when(blk + 2 < nblk)
        def _():
            far_copy(p, above).wait_recv()

        @pl.when((blk + 2 < nblk) & (odd == 0))
        def _():
            near_copy(p, slab(query_later.at[1], p)).start()

    chunks = [2 * n + c for n in (1 - x, x) for c in (1 - core_index, core_index)]
    side = others[0]
    sources = (3 - head, others[0], core)

    def source(i, b):
        if b < early or i > 1:
            return gathered.at[chunks[i], b]
        return (late_far, late)[i].at[b - early]

    def load(i, which):
        target, lo, size = ((w_out, 2 * up_cols, cols), (up, 0, up_cols), (down, up_cols, up_cols))[
            which
        ]
        return [
            pltpu.make_async_copy(
                source(i, b).at[:, pl.ds(lo, size)],
                target.at[i, pl.ds(b * part, part)],
                sems.at[which, i, b],
            )
            for b in range(nblk)
        ]

    turns = (2, 3, 1, 0)
    order = [(i, 0) for i in turns] + [(i, w) for i in turns for w in (1, 2)]
    for i, which in order:
        for b, copy in enumerate(load(i, which)):
            if i or b < early:
                copy.start()
    mixed[head] = mixed_parts[head]
    late_copy.wait()
    for which in range(3):
        for copy in load(0, which)[early:]:
            copy.start()
    for i in range(heads_of):
        for copy in load(i, 0):
            copy.wait()
    for i, to in enumerate(others):
        mixed_copy(i, to, to).wait_recv()
    branch = None
    for i in range(heads_of):
        term = dotf(mixed[chunks[i]], w_out[i], NT)
        branch = term if branch is None else branch + term
    resid = tok[...].astype(F32) + branch
    xhat, scale = statistics(resid)
    normed = (xhat * gain[...]).astype(BF16)
    cotangent = cot[...]
    total, grad_normed = resid, None

    def to_core(n, k):
        mine, theirs = ((up_grad, up_got), (down_grad, down_got), (out_grad, out_got))[k]
        return remote(mine.at[2 * n], theirs.at[n], send_c.at[k, n], recv_c.at[k, n], core, blk)

    def to_side():
        return remote(up_side, up_side_got, send_x, recv_x, side, blk)

    normed_t[...] = normed.T
    cot_t[...] = cotangent.T
    for n, i in enumerate(turns):
        for copy in load(i, 1) + load(i, 2):
            copy.wait()
        hidden, slope = gelu_both(dotf(normed, up[i]))
        hidden_all[i] = hidden.astype(BF16)
        pre_all[i] = (slope * dotf(cotangent, down[i])).astype(BF16)
        total = total + dotf(hidden_all[i], down[i], NT)
        term = dotf(pre_all[i], up[i], NT)
        grad_normed = term if grad_normed is None else grad_normed + term
        for p in range(n * pieces // heads_of, (n + 1) * pieces // heads_of):
            relay(p)
    grad = cotangent.astype(F32) + norm_back(grad_normed, xhat, scale, gain[...])
    branch_grad = grad.astype(BF16)
    lane = lax.broadcasted_iota(jnp.int32, (tok.shape[0], WIDTH), 1)

    def wide_copy(i, to, slot):
        return remote(
            wide_parts.at[to], grad_wide.at[slot], send_g.at[i], recv_g.at[i], to, blk
        )

    for i in range(heads_of):
        h = chunks[i]
        rows = dotf(branch_grad, w_out[i]).astype(BF16).astype(F32)
        product = rows * mixed[h].astype(F32)
        wide = jnp.concatenate([rows, jnp.zeros((rows.shape[0], WIDTH - cols), F32)], axis=1)
        for k in range(heads):
            delta = jnp.sum(
                product[:, k * HEAD_DIM : (k + 1) * HEAD_DIM], axis=1, keepdims=True
            )
            for c, piece in enumerate(split_parts(-delta)):
                wide = jnp.where(lane == cols + SPLITS * k + c, piece, wide)
        wide_parts[h] = wide.astype(BF16)
        if i < 3:
            wide_copy(i, h, head).start()
    grad_wide[head] = wide_parts[head]
    out[...] = total.astype(BF16)
    gain_part[...] = jnp.sum(grad_normed * xhat, axis=0, keepdims=True)
    grad_resid[...] = grad
    for i in range(heads_of):
        up_grad[i] = dotf(normed_t[...], pre_all[i]).astype(BF16)
        down_grad[i] = dotf(cot_t[...], hidden_all[i]).astype(BF16)
        if i % 2 == 0:
            to_core(i // 2, 0).start()
            to_core(i // 2, 1).start()
        if i == 1:
            to_core(0, 0).wait_recv()
            up_side[...] = (
                up_grad[1, :, :cross].astype(F32) + up_got[0, :, :cross].astype(F32)
            ).astype(BF16)
            to_side().start()
    branch_t = branch_grad.T
    for i in range(heads_of):
        out_grad[i] = dotf(branch_t, mixed[chunks[i]]).astype(BF16)
        if i % 2 == 0:
            to_core(i // 2, 2).start()

    def store(k, source, target, lo):
        size = source.shape[1]
        return [
            pltpu.make_async_copy(
                source.at[pl.ds(b * part, part)],
                target.at[b].at[:, pl.ds(lo, size)],
                out_sems.at[k, b],
            )
            for b in range(nblk)
        ]

    stores = []
    far_up = up_cols - cross
    for n, target in enumerate((give, keep)):
        at = 2 * n + 1
        for k, (mine, theirs) in enumerate(
            ((up_grad, up_got), (down_grad, down_got), (out_grad, out_got))
        ):
            if n or k:
                to_core(n, k).wait_recv()
            mine[at] = (mine[at].astype(F32) + theirs[n].astype(F32)).astype(BF16)
        stores += store(3 * n, up_grad.at[at].at[:, pl.ds(cross, far_up)], target, 0)
        stores += store(3 * n + 1, down_grad.at[at], target, far_up)
        stores += store(3 * n + 2, out_grad.at[at], target, far_up + up_cols)
        for copy in stores[-3 * nblk :]:
            copy.start()
    to_side().wait()
    up_side[...] = (up_grad[3, :, :cross].astype(F32) + up_side_got[...].astype(F32)).astype(BF16)
    stores += store(6, up_side, keep_up, 0)
    for copy in stores[-nblk:]:
        copy.start()
    for copy in stores:
        copy.wait()
    for k in range(3):
        for n in range(2):
            to_core(n, k).wait_send()
    for i in range(3):
        wide_copy(i, chunks[i], sources[i]).wait_recv()
    for i, to in enumerate(others):
        mixed_copy(i, to, head).wait_send()
        wide_copy(i, chunks[i], head).wait_send()
    for p in range(pieces):

        @pl.when((blk + 2 < nblk) | (odd == 0))
        def _():
            near_copy(p, slab(query, p)).wait_recv()

        @pl.when(blk >= 2)
        def _():
            far_copy(p, below).wait_send()

        @pl.when((blk + 2 < nblk) | (odd == 1))
        def _():
            near_copy(p, slab(query, p)).wait_send()


def middle(nblk, tok, mixed_parts, cot, gain, gathered, late, query, up_cols, cross=256, pieces=8):
    heads_of, rows, cols = mixed_parts.shape
    width, part = tok.shape[1], gathered.shape[2]
    flops = 2 * rows * width * (6 * up_cols * heads_of + 3 * width)
    dma = pltpu.SemaphoreType.DMA
    vmem = lambda *shape: pltpu.VMEM(shape, BF16)
    return pl.pallas_call(
        functools.partial(middle_kernel, nblk, up_cols, cross, pieces),
        out_shape=[
            jax.ShapeDtypeStruct((rows, width), BF16),
            jax.ShapeDtypeStruct((rows, width), F32),
            jax.ShapeDtypeStruct((heads_of, rows, WIDTH), BF16),
            jax.ShapeDtypeStruct((1, width), F32),
            jax.ShapeDtypeStruct((nblk, part, cross), BF16),
            jax.ShapeDtypeStruct((nblk, part, gathered.shape[3] - cross), BF16),
            jax.ShapeDtypeStruct((nblk, part, gathered.shape[3] - cross), BF16),
            jax.ShapeDtypeStruct((2,) + query.shape, BF16),
        ],
        in_specs=[WHOLE] * 4 + [ANY] * 3,
        out_specs=[WHOLE] * 4 + [ANY] * 4,
        scratch_shapes=[
            vmem(heads_of, width, up_cols), vmem(heads_of, width, up_cols),
            vmem(heads_of, width, cols),
            vmem(heads_of, width, up_cols), vmem(heads_of, width, up_cols),
            vmem(heads_of, width, cols),
            vmem(heads_of, rows, cols), vmem(heads_of, rows, WIDTH),
            vmem(2, width, up_cols), vmem(2, width, up_cols), vmem(2, width, cols),
            dma((3, heads_of, nblk)), dma((7, nblk)),
            dma((3,)), dma((3,)), dma((3,)), dma((3,)), dma((3, 2)), dma((3, 2)),
            dma((pieces,)), dma((pieces,)), dma((pieces,)), dma((pieces,)),
            vmem(width, cross), vmem(width, cross), dma, dma,
            vmem(heads_of, rows, up_cols), vmem(heads_of, rows, up_cols),
            vmem(width, rows), vmem(width, rows),
            vmem(*late.shape), dma, dma,
        ],
        compiler_params=pltpu.CompilerParams(
            collective_id=2, has_side_effects=True, vmem_limit_bytes=62 << 20
        ),
        cost_estimate=pl.CostEstimate(
            flops=flops, bytes_accessed=24 << 20, transcendentals=rows * up_cols * heads_of
        ),
        name="middle",
    )(tok, mixed_parts, cot, gain, gathered, late, query)


def pair_sum_kernel(up, ours, theirs, keep, give):
    odd = lax.rem(lax.axis_index("blk"), 2)
    sums = [(ours[n].astype(F32) + theirs[n].astype(F32)).astype(BF16) for n in range(2)]
    cols = up.shape[2]
    keep[0, :, :cols] = jnp.where(odd == 0, up[0], up[1])
    give[0, :, :cols] = jnp.where(odd == 0, up[1], up[0])
    keep[0, :, cols:] = jnp.where(odd == 0, sums[0], sums[1])
    give[0, :, cols:] = jnp.where(odd == 0, sums[1], sums[0])


def pair_sum(up, ours, theirs):
    nblk, part, width = ours.shape
    total = width + up.shape[2]
    spec = lambda n, cols: pl.BlockSpec((n, part, cols), lambda i: (i, 0, 0))
    return pl.pallas_call(
        pair_sum_kernel,
        grid=(nblk // 2,),
        in_specs=[spec(2, up.shape[2]), spec(2, width), spec(2, width)],
        out_specs=[spec(1, total)] * 2,
        out_shape=[jax.ShapeDtypeStruct((nblk // 2, part, total), BF16)] * 2,
        cost_estimate=pl.CostEstimate(
            flops=nblk * part * width, bytes_accessed=6 * nblk * part * width, transcendentals=0
        ),
        name="pair_sum",
    )(up, ours, theirs)


def head_rows(h, heads, shape):
    row = lax.broadcasted_iota(jnp.int32, shape, 0)
    real = heads * HEAD_DIM
    own = (row >= h * HEAD_DIM) & (row < (h + 1) * HEAD_DIM)
    return own | ((row >= real + SPLITS * h) & (row < real + SPLITS * (h + 1)))


def per_head(wide, heads, out):
    flipped = wide.T
    for h in range(heads):
        out[h] = jnp.where(head_rows(h, heads, flipped.shape), flipped, jnp.zeros_like(flipped))


def doc_start(meta, ndocs, t):
    def step(j,c):
        cum,best=c
        best=jnp.where(cum<=t,cum,best)
        return cum+meta[1+j],best
    return lax.fori_loop(0,ndocs,step,(jnp.int32(0),jnp.int32(0)),unroll=True)[1]

def doc_end(meta, ndocs, t):
    def step(j,c):
        cum,best,found=c
        cum=cum+meta[1+j]
        take=(cum>t)&(found==0)
        return cum,jnp.where(take,cum,best),jnp.where(take,1,found)
    return lax.fori_loop(0,ndocs,step,(jnp.int32(0),jnp.int32(0),jnp.int32(0)),unroll=True)[1]

def starts_vec(meta, ndocs, t):
    def step(j,c):
        cum,best=c
        return cum+meta[1+j],jnp.where(cum<=t,cum,best)
    return lax.fori_loop(0,ndocs,step,(jnp.int32(0),jnp.zeros(t.shape,jnp.int32)),unroll=True)[1]

def ends_vec(meta, ndocs, t):
    def step(j,c):
        cum,best=c
        ln=meta[1+j]
        return cum+ln,jnp.where(cum<=t,cum+ln,best)
    return lax.fori_loop(0,ndocs,step,(jnp.int32(0),jnp.zeros(t.shape,jnp.int32)),unroll=True)[1]

def widened(columns, heads):
    rows, width = columns.shape
    ones = jnp.ones((rows, SPLITS * heads), BF16)
    empty = jnp.zeros((rows, WIDTH - width - SPLITS * heads), BF16)
    return jnp.concatenate([columns, ones, empty], axis=1)


def unpack_rows(packed, heads):
    pair = 2 * HEAD_DIM
    key = jnp.concatenate([packed[:, :pair], packed[:, 2 * pair : 2 * pair + HEAD_DIM]], axis=1)
    value = jnp.concatenate([packed[:, pair : 2 * pair], packed[:, 2 * pair + HEAD_DIM :]], axis=1)
    return widened(key, heads), widened(value, heads)


STEP = 512


def build_window(heads, start, earlier, own, packed, sems, keys, values, key_rows, value_rows):
    before = earlier.shape[0] // STEP
    chunks = before + own.shape[0] // STEP

    def copy(n, source, row):
        return pltpu.make_async_copy(
            source.at[pl.ds(row * STEP, STEP)], packed.at[pl.ds(n * STEP, STEP)], sems.at[n]
        )

    def begin(n, carry):
        @pl.when(n < before)
        def _():
            copy(n, earlier, n).start()

        @pl.when(n >= before)
        def _():
            copy(n, own, n - before).start()

        return carry

    def build(n, carry):
        copy(n, own, 0).wait()
        at = pl.ds(pl.multiple_of(n * STEP, STEP), STEP)
        key, value = unpack_rows(packed[at, :], heads)
        for wide, rows, flipped in ((key, keys, key_rows), (value, values, value_rows)):
            if rows is not None:
                rows[at, :] = wide
            if flipped is not None:
                turned = wide.T
                for h in range(heads):
                    flipped[h, :HEAD_DIM, at] = turned[h * HEAD_DIM : (h + 1) * HEAD_DIM]
        return carry

    lax.fori_loop(start, chunks, begin, 0)
    lax.fori_loop(start, chunks, build, 0)


def three(lo,a,b,hi,body):
    lax.fori_loop(lo,a,lambda j,_: body(j,True),None)
    lax.fori_loop(a,b,lambda j,_: body(j,False),None)
    lax.fori_loop(b,hi,lambda j,_: body(j,True),None)

def query_tiles(meta, ndocs, t0, wbase, tq, tk):
    lo = (doc_start(meta, ndocs, t0) - wbase) // tk
    f0 = (doc_start(meta, ndocs, t0 + tq - 1) - wbase + tk - 1) // tk
    f1 = (t0 - wbase) // tk
    hi = (t0 + tq - 1 - wbase) // tk + 1
    return lo, jnp.minimum(f0, f1), f1, hi


def fwd_kernel(heads, ndocs, tq, tk, meta, q_ref, earlier, own, mix_ref, wide_ref,
               k_ref, vt_ref, qt, m_ref, acc_ref, packed, sems):
    i = pl.program_id(0)
    width = q_ref.shape[1]
    real = heads * HEAD_DIM
    base = meta[0]
    wbase = base - earlier.shape[0]

    @pl.when(i == 0)
    def _():
        vt_ref[:, HEAD_DIM:, :] = jnp.ones_like(vt_ref[:, HEAD_DIM:, :])
        start = (doc_start(meta, ndocs, base) - wbase) // tk * (tk // STEP)
        build_window(heads, start, earlier, own, packed, sems, k_ref, None, None, vt_ref)

    t0 = base + i * tq
    lo, f0, f1, hi = query_tiles(meta, ndocs, t0, wbase, tq, tk)
    q = q_ref[...]
    trow = t0 + lax.broadcasted_iota(jnp.int32, (8, tq), 1)
    srow = starts_vec(meta, ndocs, trow)[:1]
    trow = trow[:1]
    lane = lax.broadcasted_iota(jnp.int32, (tq, width), 1)

    def visible(off):
        u = wbase + off + lax.broadcasted_iota(jnp.int32, (tk, tq), 0)
        return (u >= srow) & (u <= trow)

    itself = q.astype(F32) * k_ref[pl.ds(pl.multiple_of(t0 - wbase, tq), tq), :].astype(F32)
    shifted = q.astype(F32)
    for h in range(heads):
        mine = (lane >= h * HEAD_DIM) & (lane < (h + 1) * HEAD_DIM)
        score = jnp.sum(jnp.where(mine, itself, 0.0), axis=1, keepdims=True)
        for c, piece in enumerate(split_parts(-score)):
            shifted = jnp.where(lane == real + SPLITS * h + c, piece, shifted)
    per_head(shifted.astype(BF16), heads, qt)
    acc_ref[...] = jnp.zeros_like(acc_ref)

    def quick(j, masked):
        off = pl.multiple_of(j * tk, tk)
        k = k_ref[pl.ds(off, tk), :]
        if masked:
            vis = visible(off)
        for h in range(heads):
            p = jnp.exp(dotf(k, qt[h]))
            if masked:
                p = jnp.where(vis, p, 0.0)
            acc_ref[h] += dotf(vt_ref[h, :, pl.ds(off, tk)], p.astype(BF16))

    def finish(extra):
        rows = []
        parts = []
        for h in range(heads):
            acc = acc_ref[h]
            total = acc[HEAD_DIM : HEAD_DIM + 1]
            rows.append(acc[:HEAD_DIM] / total)
            at = real + SPLITS * h
            shift = jnp.sum(qt[h, at : at + SPLITS, :].astype(F32), axis=0, keepdims=True)
            parts += split_parts(shift - extra[h] - jnp.log(total))
        rest = jnp.zeros((width - real - len(parts), tq), F32)
        turned = jnp.concatenate(rows + parts + [rest], axis=0).T
        mix_ref[0] = turned[:, :real].astype(BF16)
        wide_ref[...] = jnp.where(lane < real, q.astype(F32), turned).astype(BF16)

    three(lo, f0, f1, hi, quick)
    none = jnp.zeros((1, tq), F32)
    finish([none] * heads)
    sums = acc_ref[:, HEAD_DIM : HEAD_DIM + 1, :]
    fits = jnp.max(jnp.where(sums < 1e30, 0.0, 1.0)) == 0.0

    @pl.when(jnp.logical_not(fits))
    def _():
        acc_ref[...] = jnp.zeros_like(acc_ref)
        m_ref[...] = jnp.full_like(m_ref, EXCLUDED)

        def body(j, carry):
            off = pl.multiple_of(j * tk, tk)
            k = k_ref[pl.ds(off, tk), :]
            vis = visible(off)
            for h in range(heads):
                s = jnp.where(vis, dotf(k, qt[h]), EXCLUDED)
                old = m_ref[h, :1]
                new = jnp.maximum(old, jnp.max(s, axis=0, keepdims=True))
                m_ref[h, :1] = new
                p = jnp.exp(s - new).astype(BF16)
                acc_ref[h] = acc_ref[h] * jnp.exp(old - new) + dotf(
                    vt_ref[h, :, pl.ds(off, tk)], p
                )
            return carry

        lax.fori_loop(lo, hi, body, 0)
        finish([m_ref[h, :1] for h in range(heads)])


SCALARS = pl.BlockSpec(memory_space=pltpu.SMEM)


def attention_fwd(meta, q, earlier, own, heads, tq, tk):
    block, width = q.shape
    window = block + earlier.shape[0]
    ndocs = meta.shape[0] - 1
    return pl.pallas_call(
        functools.partial(fwd_kernel, heads, ndocs, tq, tk),
        grid=(block // tq,),
        in_specs=[
            SCALARS,
            pl.BlockSpec((tq, width), lambda i: (i, 0)),
            ANY,
            ANY,
        ],
        out_specs=[
            pl.BlockSpec((1, tq, heads * HEAD_DIM), lambda i: (i, 0, 0)),
            pl.BlockSpec((tq, width), lambda i: (i, 0)),
        ],
        out_shape=[
            jax.ShapeDtypeStruct((block // tq, tq, heads * HEAD_DIM), BF16),
            jax.ShapeDtypeStruct((block, width), BF16),
        ],
        scratch_shapes=[
            pltpu.VMEM((window, width), BF16),
            pltpu.VMEM((heads, HEAD_DIM + 16, window), BF16),
            pltpu.VMEM((heads, width, tq), BF16),
            pltpu.VMEM((heads, 8, tq), F32),
            pltpu.VMEM((heads, HEAD_DIM + 16, tq), F32),
            pltpu.VMEM((window, own.shape[1]), BF16),
            pltpu.SemaphoreType.DMA((window // STEP,)),
        ],
        compiler_params=pltpu.CompilerParams(vmem_limit_bytes=56 << 20),
        cost_estimate=pl.CostEstimate(
            flops=30_000_000_000, bytes_accessed=12 << 20, transcendentals=20_000_000
        ),
        name="attn_fwd",
    )(meta, q, earlier, own)


def dq_kernel(heads, ndocs, tq, tk, meta, q_ref, do_ref, earlier, own, dq_ref,
              k_ref, v_ref, kt_ref, qt, dot, acc_ref, packed, sems):
    i = pl.program_id(0)
    base = meta[0]
    wbase = base - earlier.shape[0]

    @pl.when(i == 0)
    def _():
        start = (doc_start(meta, ndocs, base) - wbase) // tk * (tk // STEP)
        build_window(heads, start, earlier, own, packed, sems, k_ref, v_ref, kt_ref, None)

    t0 = base + i * tq
    per_head(q_ref[...], heads, qt)
    per_head(do_ref[...], heads, dot)
    acc_ref[...] = jnp.zeros_like(acc_ref)
    trow = t0 + lax.broadcasted_iota(jnp.int32, (8, tq), 1)
    srow = starts_vec(meta, ndocs, trow)[:1]
    trow = trow[:1]

    def body(j, masked):
        off = pl.multiple_of(j * tk, tk)
        k = k_ref[pl.ds(off, tk), :]
        v = v_ref[pl.ds(off, tk), :]
        if masked:
            u = wbase + off + lax.broadcasted_iota(jnp.int32, (tk, tq), 0)
            vis = (u >= srow) & (u <= trow)
        for h in range(heads):
            p = jnp.exp(dotf(k, qt[h]))
            if masked:
                p = jnp.where(vis, p, 0.0)
            ds = (p * dotf(v, dot[h])).astype(BF16)
            acc_ref[h] += dotf(kt_ref[h, :, pl.ds(off, tk)], ds)

    three(*query_tiles(meta, ndocs, t0, wbase, tq, tk), body)
    turned = acc_ref[...].reshape(heads * HEAD_DIM, tq).T
    dq_ref[...] = (turned * (HEAD_DIM**-0.5)).astype(BF16)


def attention_dq(meta, q, do, earlier, own, heads, tq, tk):
    block, width = q.shape
    window = block + earlier.shape[0]
    ndocs = meta.shape[0] - 1
    row = lambda w: pl.BlockSpec((tq, w), lambda i: (i, 0))
    return pl.pallas_call(
        functools.partial(dq_kernel, heads, ndocs, tq, tk),
        grid=(block // tq,),
        in_specs=[SCALARS, row(width), row(width), ANY, ANY],
        out_specs=row(heads * HEAD_DIM),
        out_shape=jax.ShapeDtypeStruct((block, heads * HEAD_DIM), BF16),
        scratch_shapes=[pltpu.VMEM((window, width), BF16)] * 2
        + [pltpu.VMEM((heads, HEAD_DIM, window), BF16)]
        + [pltpu.VMEM((heads, width, tq), BF16)] * 2
        + [pltpu.VMEM((heads, HEAD_DIM, tq), F32)]
        + [pltpu.VMEM((window, own.shape[1]), BF16), pltpu.SemaphoreType.DMA((window // STEP,))],
        compiler_params=pltpu.CompilerParams(vmem_limit_bytes=56 << 20),
        cost_estimate=pl.CostEstimate(
            flops=45_000_000_000, bytes_accessed=12 << 20, transcendentals=20_000_000
        ),
        name="attn_dq",
    )(meta, q, do, earlier, own)


def dkv_kernel(heads, ndocs, tq, tk, meta, own, q_parts, do_parts, dk_ref, dv_ref,
               q_ref, do_ref, qt_ref, dot_ref, kt, vt, dk_acc, dv_acc, sems):
    i = pl.program_id(0)
    base = meta[0]

    @pl.when(i == 0)
    def _():
        block = pl.num_programs(0) * tk
        end = (doc_end(meta, ndocs, base + block - 1) - base + STEP - 1) // STEP
        sources = []
        for parts in (q_parts, do_parts):
            row, found = 0, []
            for part in parts:
                found.append((row // STEP, (row + part.shape[0]) // STEP, part))
                row += part.shape[0]
            sources.append(found)

        def copy(k, n, source, row):
            return pltpu.make_async_copy(
                source.at[pl.ds(row * STEP, STEP)],
                (q_ref, do_ref)[k].at[pl.ds(n * STEP, STEP)],
                sems.at[k, n],
            )

        def begin(n, carry):
            for k in range(2):
                for first, last, part in sources[k]:

                    @pl.when((n >= first) & (n < last))
                    def _():
                        copy(k, n, part, n - first).start()

            return carry

        def turn(n, carry):
            at = pl.ds(pl.multiple_of(n * STEP, STEP), STEP)
            for k, (rows, flipped) in enumerate(((q_ref, qt_ref), (do_ref, dot_ref))):
                copy(k, n, sources[k][0][2], 0).wait()
                turned = rows[at, :].T
                for h in range(heads):
                    flipped[h, :, at] = turned[h * HEAD_DIM : (h + 1) * HEAD_DIM]
            return carry

        lax.fori_loop(0, end, begin, 0)
        lax.fori_loop(0, end, turn, 0)

    u0 = base + i * tk
    lo = (u0 - base) // tq
    f0 = (u0 + tk - 1 - base + tq - 1) // tq
    e_first = doc_end(meta, ndocs, u0)
    e_last = doc_end(meta, ndocs, u0 + tk - 1)
    f1 = (e_first - base) // tq
    hi = (e_last - 1 - base) // tq + 1
    f0 = jnp.minimum(f0, hi)
    f1 = jnp.clip(f1, f0, hi)
    k, v = unpack_rows(own[...], heads)
    per_head(k, heads, kt)
    per_head(v, heads, vt)
    dk_acc[...] = jnp.zeros_like(dk_acc)
    dv_acc[...] = jnp.zeros_like(dv_acc)
    urow = u0 + lax.broadcasted_iota(jnp.int32, (8, tk), 1)
    erow = ends_vec(meta, ndocs, urow)[:1]
    urow = urow[:1]

    def body(j, masked):
        off = pl.multiple_of(j * tq, tq)
        at = pl.ds(off, tq)
        q = q_ref[at, :]
        do = do_ref[at, :]
        if masked:
            t = base + off + lax.broadcasted_iota(jnp.int32, (tq, tk), 0)
            vis = (t >= urow) & (t < erow)
        for h in range(heads):
            p = jnp.exp(dotf(q, kt[h]))
            if masked:
                p = jnp.where(vis, p, 0.0)
            ds = (p * dotf(do, vt[h])).astype(BF16)
            dv_acc[h] += dotf(dot_ref[h, :, at], p.astype(BF16))
            dk_acc[h] += dotf(qt_ref[h, :, at], ds)

    three(lo, f0, f1, hi, body)
    for acc, out in ((dk_acc, dk_ref), (dv_acc, dv_ref)):
        out[...] = acc[...].reshape(heads * HEAD_DIM, tk).T.astype(BF16)


def attention_dkv(meta, own, q_parts, do_parts, heads, tq, tk):
    block, width = q_parts[0].shape
    window = sum(part.shape[0] for part in q_parts)
    ndocs = meta.shape[0] - 1
    row = lambda w: pl.BlockSpec((tk, w), lambda i: (i, 0))
    return pl.pallas_call(
        functools.partial(dkv_kernel, heads, ndocs, tq, tk),
        grid=(block // tk,),
        in_specs=[SCALARS, row(own.shape[1]), [ANY] * len(q_parts), [ANY] * len(do_parts)],
        out_specs=[row(heads * HEAD_DIM)] * 2,
        out_shape=[jax.ShapeDtypeStruct((block, heads * HEAD_DIM), BF16)] * 2,
        scratch_shapes=[pltpu.VMEM((window, width), BF16)] * 2
        + [pltpu.VMEM((heads, HEAD_DIM, window), BF16)] * 2
        + [pltpu.VMEM((heads, width, tk), BF16)] * 2
        + [pltpu.VMEM((heads, HEAD_DIM, tk), F32)] * 2
        + [pltpu.SemaphoreType.DMA((2, window // STEP))],
        compiler_params=pltpu.CompilerParams(vmem_limit_bytes=56 << 20),
        cost_estimate=pl.CostEstimate(
            flops=60_000_000_000, bytes_accessed=12 << 20, transcendentals=20_000_000
        ),
        name="attn_dkv",
    )(meta, own, q_parts, do_parts)


def on_device(
    tokens, first_values, cotangent, w_query, w_key, w_value, w_out, w_up, w_down,
    gain_attn, gain_mlp, doc_lengths,
):
    width = tokens.shape[1]
    heads_of = lax.axis_size("head")
    nblk = lax.axis_size("blk")
    blk = lax.axis_index("blk")
    rows = tokens.shape[0]
    block = rows * heads_of
    heads = HEADS // heads_of
    cols = heads * HEAD_DIM
    part = width // nblk
    meta = jnp.concatenate([jnp.reshape(blk * block, (1,)).astype(jnp.int32), doc_lengths])

    up_cols = w_up.shape[1]
    early = nblk - 3 * nblk // 8
    normed, query, own, earlier, gathered, qk_all, v_all, attn_gain, mlp_gain = front(
        nblk, early, tokens, first_values, w_query, w_key, w_value, w_up, w_down.T, w_out,
        gain_attn.reshape(1, part), gain_mlp.reshape(1, part),
    )
    w_qk = qk_all.reshape(width, 2 * cols)
    w_v = v_all.reshape(2, width, w_value.shape[1])
    earlier = earlier.reshape(2 * block, 2 * cols)
    beside = [(h, (h + 2) % heads_of) for h in range(heads_of)]
    mine = lax.dynamic_index_in_dim(gathered, lax.axis_index("head"), 0, keepdims=False)[early:]
    late = lax.ppermute(mine, "head", beside)
    mixed_parts, query_wide = attention_fwd(
        meta, query, earlier, own, heads, rows, 2 * rows
    )
    late, mixed_parts = lax.optimization_barrier((late, mixed_parts))
    layer_output, grad_resid, grad_parts, gain_mlp_part, keep_up, keep, give, query_later = middle(
        nblk, tokens, mixed_parts, cotangent, mlp_gain, gathered, late, query_wide, up_cols
    )
    grad_wide = grad_parts.reshape(block, WIDTH)
    taken = lax.ppermute(give, "head", beside)

    grads_later = [grad_wide] + [
        lax.ppermute(grad_wide, "blk", [(i, i - d) for i in range(d, nblk)]) for d in (1, 2)
    ]
    queries_later = [query_wide, query_later.reshape(2 * block, WIDTH)]
    grad_query = attention_dq(
        meta, query_wide, grad_wide, earlier, own, heads, rows, 2 * rows
    )
    taken, keep, grad_query = lax.optimization_barrier((taken, keep, grad_query))
    keep, give = pair_sum(keep_up, keep, taken)
    taken = lax.ppermute(give, "blk", [(i, i + 1 - 2 * (i % 2)) for i in range(nblk)])
    keep, own = lax.optimization_barrier((keep, own))
    grad_key, grad_value = attention_dkv(
        meta, own, queries_later, grads_later, heads, rows, rows
    )
    outs = tail(
        nblk, grad_query, grad_key, grad_value, normed, w_qk, w_v, gain_mlp_part, keep, taken,
        tokens, grad_resid, attn_gain,
    )
    (
        layer_output, grad_tokens, final_query, final_key, final_value, grad_first, gain_sums,
        final_up, final_down, final_out,
    ) = settle([layer_output] + list(outs))
    return (
        layer_output,
        grad_tokens,
        grad_first,
        final_query,
        final_key,
        final_value,
        final_out,
        final_up,
        final_down.T,
        gain_sums[0].reshape(part),
        gain_sums[1].reshape(part),
    )


def solution(mesh):
    rows = P(("blk", "head"), None)
    specs = (P("blk", "head"),) * 3 + (P("head", "blk"), P("blk", "head"), P("head", "blk"))
    gains = (P("blk"), P("blk"))
    return jax.shard_map(
        on_device,
        mesh=mesh,
        in_specs=(rows,) * 3 + specs + gains + (P(),),
        out_specs=(rows,) * 3 + specs + gains,
        check_vma=False,
    )
```

profile of v0, /device:TPU:0, one launch (start us, length us, event | category | flops | bytes accessed | tf_op | source)
XLA Modules:
  0.0 366.2 jit_solution(1766857576536809603)
XLA Ops:
  0.6 0.0 copy-start.4
  0.7 88.5 %front.1 = (bf16[2048,768]{1,0:T(8,128)(2,1)}, bf16[2048,256]{1,0:T(8,128)(2,1)}, bf16[2048,384]{1,0:T(8,128)(2,1)}, bf16[2,2048,384]{2,1,0:T(8,128)(2,1)}, bf16...) custom-call(bf16[512,768]{1,0:T(8,128)(2,1)} %tok.5, ...), custom_call_target="tpu_custom_call" | custom-call | tf_op jit(solution)/shard_map/front/pallas_call | solution.py:798
  89.1 1.3 dynamic-slice_bitcast_fusion
  90.4 3.0 collective-permute-start
  93.5 0.0 copy-done.4
  93.5 0.6 pad_add_fusion.meta
  94.0 17.0 %attn_fwd.1 = (bf16[4,512,192]{2,1,0:T(8,128)(2,1)}, bf16[2048,256]{1,0:T(8,128)(2,1)}) custom-call(s32[17]{0:T(128)} %pad_add_fusion.meta, bf16[2048,256]{1,0:T(8,128)(2,1)} %get-tuple-element.61.q_ref, bf16[4096,384]{1,0:T(8,128)(2,1)} %bitcast.21, bf16[2048,384]{1,0:T(8,128)(2,1)} %get-tuple-element.78.own), custom_call_target="tpu_custom_call" | custom-call | flops 30000001024 | bytes 12582912 | tf_op jit(solution)/shard_map/attn_fwd/pallas_call | solution.py:1356
  111.1 5.3 %collective-permute-done.late = bf16[3,96,1728]{2,1,0:T(8,128)(2,1)S(1)} collective-permute-done((bf16[3,96,1728]{2,1,0:T(8,128)(2,1)S(1)}, bf16[3,96,1728]{2,1,0:T(8,128)(2,1)S(1)}, u32[]{:S(2)}, u32[]{:S(2)}) %collective-permute-start) | collective-permute-done | bytes 995360 | tf_op jit(solution)/shard_map/ppermute | solution.py:1587
  116.4 0.0 copy-start.3
  116.4 1.0 copy-done.3
  117.4 67.7 %middle.1 = (bf16[512,768]{1,0:T(8,128)(2,1)}, f32[512,768]{1,0:T(8,128)}, bf16[4,512,256]{2,1,0:T(8,128)(2,1)}, f32[1,768]{1,0:T(1,128)}, bf16[8,96,256]{2,1,0:...) custom-call(bf16[512,768]{1,0:T(8,128)(2,1)} %tok.5, ...), custom_call_target="tpu_custom_call" | custom-call | flops 16307453952 | bytes 25165824 | tf_op jit(solution)/shard_map/middle/pallas_call | solution.py:1083
  185.1 1.3 collective-permute-start.3
  186.4 1.3 collective-permute-start.2
  187.7 0.1 collective-permute-start.1
  187.8 22.2 %attn_dq.1.d_q = bf16[2048,192]{1,0:T(8,128)(2,1)} custom-call(s32[17]{0:T(128)} %pad_add_fusion.meta, bf16[2048,256]{1,0:T(8,128)(2,1)} %get-tuple-element.68.query.q_ref.q_parts_0_, bf16[2048,256]{1,0:T(8,128)(2,1)} %bitcast.25, bf16[4096,384]{1,0:T(8,128)(2,1)} %bitcast.22, bf16[2048,384]{1,0:T(8,128)(2,1)} %get-tuple-element.78.own), custom_call_target="tpu_custom_call" | custom-call | flops 44999999488 | bytes 12582912 | tf_op jit(solution)/shard_map/attn_dq/pallas_call | solution.py:1433
  210.0 30.7 %collective-permute-done.1.theirs = bf16[8,96,1472]{2,1,0:T(8,128)(2,1)S(1)} collective-permute-done((bf16[8,96,1472]{2,1,0:T(8,128)(2,1)}, bf16[8,96,1472]{2,1,0:T(8,128)(2,1)S(1)}, u32[]{:S(2)}, u32[]{:S(2)}) %collective-permute-start.1) | collective-permute-done | bytes 2261024 | tf_op jit(solution)/shard_map/ppermute | solution.py:1596
  240.7 0.0 copy-start
  240.7 1.4 copy-done
  242.1 4.7 %pair_sum.1 = (bf16[4,96,1728]{2,1,0:T(8,128)(2,1)}, bf16[4,96,1728]{2,1,0:T(8,128)(2,1)}) custom-call(bf16[8,96,256]{2,1,0:T(8,128)(2,1)} %get-tuple-element.74.up, bf16[8,96,1472]{2,1,0:T(8,128)(2,1)} %get-tuple-element.75.ours, bf16[8,96,1472]{2,1,0:T(8,128)(2,1)} %copy-done), custom_call_target="tpu_custom_call" | custom-call | flops 1130496 | bytes 6782976 | tf_op jit(solution)/shard_map/pair_sum/pallas_call | solution.py:1136
  246.8 3.0 collective-permute-start.4
  249.8 0.0 collective-permute-done.3.do_parts_2_
  249.8 0.0 copy-start.2
  249.8 0.0 collective-permute-done.2.do_parts_1_
  249.8 1.0 copy-done.2
  250.7 49.7 %attn_dkv.1 = (bf16[2048,192]{1,0:T(8,128)(2,1)}, bf16[2048,192]{1,0:T(8,128)(2,1)}) custom-call(s32[17]{0:T(128)} %pad_add_fusion.meta, bf16[2048,384]{1,0:T(8,128)(2,1)} %get-tuple-element.78.own, bf16[2048,256]{1,0:T(8,128)(2,1)} %get-tuple-element.68.query.q_ref.q_parts_0_, bf16[4096,256]{1,0:T(8,128)(2,1)} %bitcast.28, bf16[2048,256]{1,0:T(8,128)(2,1)} %bitcast.26, ...), custom_call_target="tpu_custom_call" | custom-call | flops 60000002048 | bytes 12582912 | tf_op jit(solution)/shard_map/attn_dkv/pallas_call | solution.py:1542
  300.5 0.0 collective-permute-done.4.got
  300.5 0.0 copy-start.1
  300.5 1.1 copy-done.1
  301.6 58.8 %tail.1 = (f32[512,768]{1,0:T(8,128)}, f32[96,192]{1,0:T(8,128)}, f32[96,192]{1,0:T(8,128)}, f32[96,96]{1,0:T(8,128)}, f32[512,384]{1,0:T(8,128)}, /*index=5*/f3...) custom-call(bf16[2048,192]{1,0:T(8,128)(2,1)} %attn_dq.1.d_q, ...), custom_call_target="tpu_custom_call" | custom-call | tf_op jit(solution)/shard_map/tail/pallas_call | solution.py:436
  360.3 4.2 %settle.1 = (bf16[512,768]{1,0:T(8,128)(2,1)}, f32[512,768]{1,0:T(8,128)}, f32[96,192]{1,0:T(8,128)}, f32[96,192]{1,0:T(8,128)}, f32[96,96]{1,0:T(8,128)}, /*ind...) custom-call(bf16[512,768]{1,0:T(8,128)(2,1)} %get-tuple-element.69.refs_0, ...), custom_call_target="tpu_custom_call" | custom-call | tf_op jit(solution)/shard_map/settle/pallas_call | solution.py:495
  364.5 1.2 slice_bitcast_fusion
Async XLA Ops:
  0.6 92.8 %copy-start.4 = (s32[16]{0:T(128)S(1)}, s32[16]{0:T(128)}, u32[]{:S(2)}) copy-start(s32[16]{0:T(128)} %param.23) | copy-start | bytes 196
  90.4 26.0 %collective-permute-start = (bf16[3,96,1728]{2,1,0:T(8,128)(2,1)S(1)}, bf16[3,96,1728]{2,1,0:T(8,128)(2,1)S(1)}, u32[]{:S(2)}, u32[]{:S(2)}) collective-permute-start(bf16[3,96,1728]{2,1,0:T(8,128)(2,1)S(1)} %dynamic-slice_bitcast_fusion), channel_id=1, source_target_pairs={{0,16},{8,24},{16,0},{24,8},{1,17},{9,25},{17,1},{25,9},{2,18},{10... | collective-permute-start | bytes 2985992 | tf_op jit(solution)/shard_map/ppermute | solution.py:1587
  116.4 1.0 copy-start.3
  185.1 64.7 %collective-permute-start.3 = (bf16[2048,256]{1,0:T(8,128)(2,1)}, bf16[2048,256]{1,0:T(8,128)(2,1)S(1)}, u32[]{:S(2)}, u32[]{:S(2)}) collective-permute-start(bf16[2048,256]{1,0:T(8,128)(2,1)} %bitcast.23), channel_id=1, source_target_pairs={{2,0},{3,1},{4,2},{5,3},{6,4},{7,5},{10,8},{11,9},{12,10},{13,11},... | collective-permute-start | bytes 3145736 | tf_op jit(solution)/shard_map/ppermute | solution.py:1599
  186.4 63.4 %collective-permute-start.2 = (bf16[2048,256]{1,0:T(8,128)(2,1)}, bf16[2048,256]{1,0:T(8,128)(2,1)}, u32[]{:S(2)}, u32[]{:S(2)}) collective-permute-start(bf16[2048,256]{1,0:T(8,128)(2,1)} %bitcast.24), channel_id=1, source_target_pairs={{1,0},{2,1},{3,2},{4,3},{5,4},{6,5},{7,6},{9,8},{10,9},{11,10},{12... | collective-permute-start | bytes 3145736 | tf_op jit(solution)/shard_map/ppermute | solution.py:1599
  187.7 53.0 %collective-permute-start.1 = (bf16[8,96,1472]{2,1,0:T(8,128)(2,1)}, bf16[8,96,1472]{2,1,0:T(8,128)(2,1)S(1)}, u32[]{:S(2)}, u32[]{:S(2)}) collective-permute-start(bf16[8,96,1472]{2,1,0:T(8,128)(2,1)} %get-tuple-element.70), channel_id=1, source_target_pairs={{0,16},{8,24},{16,0},{24,8},{1,17},{9,25},{17,1},{25,9},{2,18},{10... | collective-permute-start | bytes 6782984 | tf_op jit(solution)/shard_map/ppermute | solution.py:1596
  240.7 1.4 copy-start
  246.8 53.7 %collective-permute-start.4 = (bf16[4,96,1728]{2,1,0:T(8,128)(2,1)}, bf16[4,96,1728]{2,1,0:T(8,128)(2,1)S(1)}, u32[]{:S(2)}, u32[]{:S(2)}) collective-permute-start(bf16[4,96,1728]{2,1,0:T(8,128)(2,1)} %get-tuple-element.87), channel_id=1, source_target_pairs={{0,1},{1,0},{2,3},{3,2},{4,5},{5,4},{6,7},{7,6},{8,9},{9,8},{10,11... | collective-permute-start | bytes 3981320 | tf_op jit(solution)/shard_map/ppermute | solution.py:1607
  249.8 1.0 copy-start.2
  300.5 1.1 copy-start.1
where the time goes:
time: 371 us; the launch traced here: 366 us
  Pallas kernels  313 us (84%)
  waiting for transfers between devices  36 us (10%)
  starting transfers between devices  8.65 us (2%)
  local copies, waits for them, and re-layouts  6.97 us (2%)
    pallas_call x1, Pallas kernels, front(): pl.pallas_call(functools.partial(front_kernel, nblk, parts, pieces, early...  88.5 us
    pallas_call x1, Pallas kernels, middle(): pl.pallas_call(functools.partial(middle_kernel, nblk, up_cols, cross, pie...  67.7 us
    pallas_call x1, Pallas kernels, tail(): pl.pallas_call(functools.partial(tail_kernel, nblk, pieces, cols), out_sh...  58.8 us
    pallas_call x1, Pallas kernels, attention_dkv(): pl.pallas_call(functools.partial(dkv_kernel, heads, ndocs, tq, tk), grid=...  49.7 us
    ppermute x1, waiting for transfers between devices, on_device(): taken = lax.ppermute(give, 'head', beside)  30.7 us
    pallas_call x1, Pallas kernels, attention_dq(): pl.pallas_call(functools.partial(dq_kernel, heads, ndocs, tq, tk), grid=(...  22.2 us
    pallas_call x1, Pallas kernels, attention_fwd(): pl.pallas_call(functools.partial(fwd_kernel, heads, ndocs, tq, tk), grid=...  17 us
  transfers between devices with their start and end apart: 5, of which 2 were waited for; matrix products, arithmetic and copies ran while one was open for 0% of the time, Pallas kernels for 26%

commit v1 on v0

--- a/solution.py
+++ b/solution.py
@@ -147,7 +147,7 @@
 
 
 def tail_kernel(
-    nblk, pieces, cols, d_q, d_k, d_v, normed, w_qk, w_v, gain_m, kept, got, tok, resid, gain,
+    nblk, pieces, cols, d_q, d_k, d_v, normed, w_qk, w_v, gain_m, kept_a, got_a, kept_b, got_b, tok, resid, gain,
     out_grad, out_q, out_k, out_v, out_first, out_gain, out_up, out_down, out_out,
     grad, weights, gains, joined, weight, acc, first_got, rest_sum,
     core_buf, side_out, side_buf, pair_buf, line_out, line_in, v_sum, v_got,
@@ -178,7 +178,8 @@
         )
 
     def sum_of(t):
-        return kept[t].astype(F32) + got[t].astype(F32)
+        first_part = kept_b[t].astype(F32) + got_b[t].astype(F32)
+        return jnp.concatenate([first_part, kept_a[t].astype(F32) + got_a[t].astype(F32)], axis=1)
 
     def up_copy(t, to):
         return remote(up_out.at[t], up_in.at[t], send_u.at[t], recv_u.at[t], head, to)
@@ -361,8 +362,10 @@
             rest_sum[...] += down_in[t].astype(F32)
 
     inner = out_up.shape[1]
-    out_up[...] = rest_sum[:, :inner]
-    out_down[...] = rest_sum[:, inner : 2 * inner]
+    cut = kept_b.shape[2]
+    out_up[...] = rest_sum[:, cut : cut + inner]
+    out_down[:, :cut] = rest_sum[:, :cut]
+    out_down[:, cut:] = rest_sum[:, cut + inner : 2 * inner]
     out_out[...] = rest_sum[:, 2 * inner :].T
     for i, to in enumerate(peers):
         gain_copy(i, to).wait_recv()
@@ -424,10 +427,14 @@
             down_copy(t, below).wait_send()
 
 
-def tail(nblk, d_q, d_k, d_v, normed, w_qk, w_v, gain_m, kept, got, tok, resid, gain, pieces=4):
+def tail(
+    nblk, d_q, d_k, d_v, normed, w_qk, w_v, gain_m, kept_a, got_a, kept_b, got_b, tok, resid, gain,
+    pieces=4,
+):
     dma = pltpu.SemaphoreType.DMA
     row, part, cols = tok.shape, w_v.shape[1] // nblk, d_q.shape[1]
-    inner = (kept.shape[2] - cols) // 2
+    rest = (nblk // 2, part, kept_a.shape[2] + kept_b.shape[2])
+    inner = (rest[2] - cols) // 2
     padded = -(-3 * cols // 128) * 128
     gains = jax.ShapeDtypeStruct((nblk, 2, 1, part), F32)
     half, line = (part, cols // 2), nblk // 2
@@ -446,12 +453,12 @@
             jax.ShapeDtypeStruct((part, inner), F32),
             jax.ShapeDtypeStruct((cols, part), F32),
         ],
-        in_specs=[WHOLE] * 12,
+        in_specs=[WHOLE] * 14,
         out_specs=[WHOLE] * 9,
         scratch_shapes=[
             vmem(4, *row), vmem(nblk, part, padded), pltpu.VMEM(gains.shape, F32),
             vmem(row[0], padded), vmem(row[1], 3 * cols), pltpu.VMEM((row[1], padded), F32),
-            vmem(2, row[0], cols), pltpu.VMEM(kept.shape[1:], F32),
+            vmem(2, row[0], cols), pltpu.VMEM(rest[1:], F32),
             vmem(2, *row), vmem(*row), vmem(*row),
             vmem(line, part, padded), vmem(line, part, padded),
             vmem(line, part, padded),
@@ -460,7 +467,7 @@
             pltpu.VMEM(gains.shape, F32),
             pltpu.VMEM(gains.shape[1:], F32),
             pltpu.VMEM((3,) + gains.shape[1:], F32),
-            vmem(*kept.shape), vmem(*kept.shape), vmem(*kept.shape), vmem(*kept.shape),
+            vmem(*rest), vmem(*rest), vmem(*rest), vmem(*rest),
             dma,
             dma(piece), dma(piece),
             dma((pieces,)), dma((pieces,)),
@@ -475,7 +482,7 @@
             collective_id=4, has_side_effects=True, vmem_limit_bytes=60 << 20
         ),
         name="tail",
-    )(d_q, d_k, d_v, normed, w_qk, w_v, gain_m, kept, got, tok, resid, gain)
+    )(d_q, d_k, d_v, normed, w_qk, w_v, gain_m, kept_a, got_a, kept_b, got_b, tok, resid, gain)
 
 
 def settle_kernel(count, *refs):
@@ -845,11 +852,11 @@
 
 
 def middle_kernel(
-    nblk, up_cols, cross, pieces, tok, mixed_parts, cot, gain, gathered, late, query,
-    out, grad_resid, grad_wide, gain_part, keep_up, keep, give, query_later,
+    nblk, up_cols, cut, pieces, tok, mixed_parts, cot, gain, gathered, late, query,
+    out, grad_resid, grad_wide, gain_part, keep_a, give_a, keep_b, give_b, query_later,
     up, down, w_out, up_grad, down_grad, out_grad, mixed, wide_parts, up_got, down_got, out_got,
     sems, out_sems, send_m, recv_m, send_g, recv_g, send_c, recv_c,
-    send_z, recv_z, send_y, recv_y, up_side, up_side_got, send_x, recv_x, hidden_all, pre_all, normed_t, cot_t, late_far, send_l, recv_l,
+    send_z, recv_z, send_y, recv_y, hidden_all, pre_all, normed_t, cot_t, late_far, send_l, recv_l,
 ):
     head, blk = lax.axis_index("head"), lax.axis_index("blk")
     x, core_index = lax.div(head, 2), lax.rem(head, 2)
@@ -957,9 +964,6 @@
         mine, theirs = ((up_grad, up_got), (down_grad, down_got), (out_grad, out_got))[k]
         return remote(mine.at[2 * n], theirs.at[n], send_c.at[k, n], recv_c.at[k, n], core, blk)
 
-    def to_side():
-        return remote(up_side, up_side_got, send_x, recv_x, side, blk)
-
     normed_t[...] = normed.T
     cot_t[...] = cotangent.T
     for n, i in enumerate(turns):
@@ -1006,12 +1010,6 @@
         if i % 2 == 0:
             to_core(i // 2, 0).start()
             to_core(i // 2, 1).start()
-        if i == 1:
-            to_core(0, 0).wait_recv()
-            up_side[...] = (
-                up_grad[1, :, :cross].astype(F32) + up_got[0, :, :cross].astype(F32)
-            ).astype(BF16)
-            to_side().start()
     branch_t = branch_grad.T
     for i in range(heads_of):
         out_grad[i] = dotf(branch_t, mixed[chunks[i]]).astype(BF16)
@@ -1023,32 +1021,39 @@
         return [
             pltpu.make_async_copy(
                 source.at[pl.ds(b * part, part)],
-                target.at[b].at[:, pl.ds(lo, size)],
+                target(b).at[:, pl.ds(lo, size)],
                 out_sems.at[k, b],
             )
             for b in range(nblk)
         ]
 
     stores = []
-    far_up = up_cols - cross
-    for n, target in enumerate((give, keep)):
+    for n, target in enumerate((give_a, keep_a)):
         at = 2 * n + 1
         for k, (mine, theirs) in enumerate(
             ((up_grad, up_got), (down_grad, down_got), (out_grad, out_got))
         ):
-            if n or k:
-                to_core(n, k).wait_recv()
+            to_core(n, k).wait_recv()
             mine[at] = (mine[at].astype(F32) + theirs[n].astype(F32)).astype(BF16)
-        stores += store(3 * n, up_grad.at[at].at[:, pl.ds(cross, far_up)], target, 0)
-        stores += store(3 * n + 1, down_grad.at[at], target, far_up)
-        stores += store(3 * n + 2, out_grad.at[at], target, far_up + up_cols)
-        for copy in stores[-3 * nblk :]:
+        first_part = store(3 * n, up_grad.at[at], lambda b: target.at[b], 0)
+        far_down = down_grad.at[at].at[:, pl.ds(cut, up_cols - cut)]
+        first_part += store(6 + n, far_down, lambda b: target.at[b], up_cols)
+        first_part += store(3 * n + 1, out_grad.at[at], lambda b: target.at[b], 2 * up_cols - cut)
+        for copy in first_part:
             copy.start()
-    to_side().wait()
-    up_side[...] = (up_grad[3, :, :cross].astype(F32) + up_side_got[...].astype(F32)).astype(BF16)
-    stores += store(6, up_side, keep_up, 0)
-    for copy in stores[-nblk:]:
-        copy.start()
+        kept = store(3 * n + 2, down_grad.at[at].at[:, pl.ds(0, cut)], lambda b: keep_b.at[n, b // 2], 0)
+        given = store(3 * n + 2, down_grad.at[at].at[:, pl.ds(0, cut)], lambda b: give_b.at[n, b // 2], 0)
+        for b in range(nblk):
+
+            @pl.when(odd == b % 2)
+            def _():
+                kept[b].start()
+
+            @pl.when(odd != b % 2)
+            def _():
+                given[b].start()
+
+        stores += first_part + kept
     for copy in stores:
         copy.wait()
     for k in range(3):
@@ -1074,26 +1079,27 @@
             near_copy(p, slab(query, p)).wait_send()
 
 
-def middle(nblk, tok, mixed_parts, cot, gain, gathered, late, query, up_cols, cross=256, pieces=8):
+def middle(nblk, tok, mixed_parts, cot, gain, gathered, late, query, up_cols, cut=512, pieces=8):
     heads_of, rows, cols = mixed_parts.shape
     width, part = tok.shape[1], gathered.shape[2]
     flops = 2 * rows * width * (6 * up_cols * heads_of + 3 * width)
     dma = pltpu.SemaphoreType.DMA
     vmem = lambda *shape: pltpu.VMEM(shape, BF16)
     return pl.pallas_call(
-        functools.partial(middle_kernel, nblk, up_cols, cross, pieces),
+        functools.partial(middle_kernel, nblk, up_cols, cut, pieces),
         out_shape=[
             jax.ShapeDtypeStruct((rows, width), BF16),
             jax.ShapeDtypeStruct((rows, width), F32),
             jax.ShapeDtypeStruct((heads_of, rows, WIDTH), BF16),
             jax.ShapeDtypeStruct((1, width), F32),
-            jax.ShapeDtypeStruct((nblk, part, cross), BF16),
-            jax.ShapeDtypeStruct((nblk, part, gathered.shape[3] - cross), BF16),
-            jax.ShapeDtypeStruct((nblk, part, gathered.shape[3] - cross), BF16),
+            jax.ShapeDtypeStruct((nblk, part, 2 * up_cols - cut + cols), BF16),
+            jax.ShapeDtypeStruct((nblk, part, 2 * up_cols - cut + cols), BF16),
+            jax.ShapeDtypeStruct((2, nblk // 2, part, cut), BF16),
+            jax.ShapeDtypeStruct((2, nblk // 2, part, cut), BF16),
             jax.ShapeDtypeStruct((2,) + query.shape, BF16),
         ],
         in_specs=[WHOLE] * 4 + [ANY] * 3,
-        out_specs=[WHOLE] * 4 + [ANY] * 4,
+        out_specs=[WHOLE] * 4 + [ANY] * 5,
         scratch_shapes=[
             vmem(heads_of, width, up_cols), vmem(heads_of, width, up_cols),
             vmem(heads_of, width, cols),
@@ -1101,10 +1107,9 @@
             vmem(heads_of, width, cols),
             vmem(heads_of, rows, cols), vmem(heads_of, rows, WIDTH),
             vmem(2, width, up_cols), vmem(2, width, up_cols), vmem(2, width, cols),
-            dma((3, heads_of, nblk)), dma((7, nblk)),
+            dma((3, heads_of, nblk)), dma((8, nblk)),
             dma((3,)), dma((3,)), dma((3,)), dma((3,)), dma((3, 2)), dma((3, 2)),
             dma((pieces,)), dma((pieces,)), dma((pieces,)), dma((pieces,)),
-            vmem(width, cross), vmem(width, cross), dma, dma,
             vmem(heads_of, rows, up_cols), vmem(heads_of, rows, up_cols),
             vmem(width, rows), vmem(width, rows),
             vmem(*late.shape), dma, dma,
@@ -1119,31 +1124,33 @@
     )(tok, mixed_parts, cot, gain, gathered, late, query)
 
 
-def pair_sum_kernel(up, ours, theirs, keep, give):
+def pair_sum_kernel(ours_a, got_a, ours_b, got_b, keep_a, give_a, keep_b, give_b):
     odd = lax.rem(lax.axis_index("blk"), 2)
-    sums = [(ours[n].astype(F32) + theirs[n].astype(F32)).astype(BF16) for n in range(2)]
-    cols = up.shape[2]
-    keep[0, :, :cols] = jnp.where(odd == 0, up[0], up[1])
-    give[0, :, :cols] = jnp.where(odd == 0, up[1], up[0])
-    keep[0, :, cols:] = jnp.where(odd == 0, sums[0], sums[1])
-    give[0, :, cols:] = jnp.where(odd == 0, sums[1], sums[0])
-
-
-def pair_sum(up, ours, theirs):
-    nblk, part, width = ours.shape
-    total = width + up.shape[2]
-    spec = lambda n, cols: pl.BlockSpec((n, part, cols), lambda i: (i, 0, 0))
+    sums = [(ours_a[n].astype(F32) + got_a[n].astype(F32)).astype(BF16) for n in range(2)]
+    keep_a[0] = jnp.where(odd == 0, sums[0], sums[1])
+    give_a[0] = jnp.where(odd == 0, sums[1], sums[0])
+    give_b[0] = (ours_b[0, 0].astype(F32) + got_b[0, 0].astype(F32)).astype(BF16)
+    keep_b[0] = (ours_b[1, 0].astype(F32) + got_b[1, 0].astype(F32)).astype(BF16)
+
+
+def pair_sum(ours_a, got_a, ours_b, got_b):
+    nblk, part, width = ours_a.shape
+    other = ours_b.shape[3]
+    a_in = pl.BlockSpec((2, part, width), lambda i: (i, 0, 0))
+    b_in = pl.BlockSpec((2, 1, part, other), lambda i: (0, i, 0, 0))
+    out = lambda cols: pl.BlockSpec((1, part, cols), lambda i: (i, 0, 0))
+    shape = lambda cols: jax.ShapeDtypeStruct((nblk // 2, part, cols), BF16)
     return pl.pallas_call(
         pair_sum_kernel,
         grid=(nblk // 2,),
-        in_specs=[spec(2, up.shape[2]), spec(2, width), spec(2, width)],
-        out_specs=[spec(1, total)] * 2,
-        out_shape=[jax.ShapeDtypeStruct((nblk // 2, part, total), BF16)] * 2,
+        in_specs=[a_in, a_in, b_in, b_in],
+        out_specs=[out(width)] * 2 + [out(other)] * 2,
+        out_shape=[shape(width)] * 2 + [shape(other)] * 2,
         cost_estimate=pl.CostEstimate(
-            flops=nblk * part * width, bytes_accessed=6 * nblk * part * width, transcendentals=0
+            flops=nblk * part * width, bytes_accessed=12 * nblk * part * width, transcendentals=0
         ),
         name="pair_sum",
-    )(up, ours, theirs)
+    )(ours_a, got_a, ours_b, got_b)
 
 
 def head_rows(h, heads, shape):
@@ -1589,11 +1596,13 @@
         meta, query, earlier, own, heads, rows, 2 * rows
     )
     late, mixed_parts = lax.optimization_barrier((late, mixed_parts))
-    layer_output, grad_resid, grad_parts, gain_mlp_part, keep_up, keep, give, query_later = middle(
+    layer_output, grad_resid, grad_parts, gain_mlp_part, keep_a, give_a, keep_b, give_b, query_later = middle(
         nblk, tokens, mixed_parts, cotangent, mlp_gain, gathered, late, query_wide, up_cols
     )
     grad_wide = grad_parts.reshape(block, WIDTH)
-    taken = lax.ppermute(give, "head", beside)
+    across = [(i, i + 1 - 2 * (i % 2)) for i in range(nblk)]
+    got_a = lax.ppermute(give_a, "head", beside)
+    got_b = lax.ppermute(give_b, "blk", across)
 
     grads_later = [grad_wide] + [
         lax.ppermute(grad_wide, "blk", [(i, i - d) for i in range(d, nblk)]) for d in (1, 2)
@@ -1602,16 +1611,17 @@
     grad_query = attention_dq(
         meta, query_wide, grad_wide, earlier, own, heads, rows, 2 * rows
     )
-    taken, keep, grad_query = lax.optimization_barrier((taken, keep, grad_query))
-    keep, give = pair_sum(keep_up, keep, taken)
-    taken = lax.ppermute(give, "blk", [(i, i + 1 - 2 * (i % 2)) for i in range(nblk)])
-    keep, own = lax.optimization_barrier((keep, own))
+    got_a, got_b, grad_query = lax.optimization_barrier((got_a, got_b, grad_query))
+    keep_a, give_a, keep_b, give_b = pair_sum(keep_a, got_a, keep_b, got_b)
+    got_a = lax.ppermute(give_a, "blk", across)
+    got_b = lax.ppermute(give_b, "head", beside)
+    keep_a, own = lax.optimization_barrier((keep_a, own))
     grad_key, grad_value = attention_dkv(
         meta, own, queries_later, grads_later, heads, rows, rows
     )
     outs = tail(
-        nblk, grad_query, grad_key, grad_value, normed, w_qk, w_v, gain_mlp_part, keep, taken,
-        tokens, grad_resid, attn_gain,
+        nblk, grad_query, grad_key, grad_value, normed, w_qk, w_v, gain_mlp_part,
+        keep_a, got_a, keep_b, got_b, tokens, grad_resid, attn_gain,
     )
     (
         layer_output, grad_tokens, final_query, final_key, final_value, grad_first, gain_sums,

time: 371 us -> 347 us (0.935); the launches traced: 366 us -> 348 us
  Pallas kernels: 313 us -> 302 us
  waiting for transfers between devices: 36 us -> 27.8 us
    ppermute x2 -> x4, waiting for transfers between devices: 30.7 us -> 22.5 us  [the longest x1 17.6 us: on_device(): got_b = lax.ppermute(give_b, 'blk', across)]
    pallas_call x1, Pallas kernels: 58.8 us -> 51.6 us  [tail(): pl.pallas_call(functools.partial(tail_kernel, nblk, pieces, cols), out_sh...]
    pallas_call x2, Pallas kernels: 72.3 us -> 68.3 us  [the longest x1 63.7 us: middle(): pl.pallas_call(functools.partial(middle_kernel, nblk, up_cols, cut, piece...]
  transfers between devices with their start and end apart: 5 -> 7, of which waited for: 2 -> 3; matrix products, arithmetic and copies ran while one was open for 0% -> 0% of each run, Pallas kernels for 26% -> 27%
where the time goes in v1:
time: 347 us; the launch traced here: 348 us
  Pallas kernels  302 us (87%)
  waiting for transfers between devices  27.8 us (8%)
  starting transfers between devices  10.5 us (3%)
  local copies, waits for them, and re-layouts  5.88 us (2%)
    pallas_call x1, Pallas kernels, front(): pl.pallas_call(functools.partial(front_kernel, nblk, parts, pieces, early...  88.5 us
    pallas_call x1, Pallas kernels, middle(): pl.pallas_call(functools.partial(middle_kernel, nblk, up_cols, cut, piece...  63.7 us
    pallas_call x1, Pallas kernels, tail(): pl.pallas_call(functools.partial(tail_kernel, nblk, pieces, cols), out_sh...  51.6 us
    pallas_call x1, Pallas kernels, attention_dkv(): pl.pallas_call(functools.partial(dkv_kernel, heads, ndocs, tq, tk), grid=...  49.7 us
    pallas_call x1, Pallas kernels, attention_dq(): pl.pallas_call(functools.partial(dq_kernel, heads, ndocs, tq, tk), grid=(...  22.2 us
    ppermute x1, waiting for transfers between devices, on_device(): got_b = lax.ppermute(give_b, 'blk', across)  17.6 us
    pallas_call x1, Pallas kernels, attention_fwd(): pl.pallas_call(functools.partial(fwd_kernel, heads, ndocs, tq, tk), grid=...  17 us
  transfers between devices with their start and end apart: 7, of which 3 were waited for; matrix products, arithmetic and copies ran while one was open for 0% of the time, Pallas kernels for 27%

profile of v1, /device:TPU:0, one launch (start us, length us, event | category | flops | bytes accessed | tf_op | source)
XLA Modules:
  0.0 347.6 jit_solution(16976877528249078714)
XLA Ops:
  0.6 0.0 copy-start.5
  0.7 88.5 %front.1 = (bf16[2048,768]{1,0:T(8,128)(2,1)}, bf16[2048,256]{1,0:T(8,128)(2,1)}, bf16[2048,384]{1,0:T(8,128)(2,1)}, bf16[2,2048,384]{2,1,0:T(8,128)(2,1)}, bf16...) custom-call(bf16[512,768]{1,0:T(8,128)(2,1)} %tok.5, ...), custom_call_target="tpu_custom_call" | custom-call | tf_op jit(solution)/shard_map/front/pallas_call | solution.py:805
  89.2 1.3 dynamic-slice_bitcast_fusion
  90.5 3.0 collective-permute-start
  93.5 0.0 copy-done.5
  93.5 0.6 pad_add_fusion.meta
  94.1 17.0 %attn_fwd.1 = (bf16[4,512,192]{2,1,0:T(8,128)(2,1)}, bf16[2048,256]{1,0:T(8,128)(2,1)}) custom-call(s32[17]{0:T(128)} %pad_add_fusion.meta, bf16[2048,256]{1,0:T(8,128)(2,1)} %get-tuple-element.64.q_ref, bf16[4096,384]{1,0:T(8,128)(2,1)} %bitcast.21, bf16[2048,384]{1,0:T(8,128)(2,1)} %get-tuple-element.82.own), custom_call_target="tpu_custom_call" | custom-call | flops 30000001024 | bytes 12582912 | tf_op jit(solution)/shard_map/attn_fwd/pallas_call | solution.py:1363
  111.1 5.3 %collective-permute-done.late = bf16[3,96,1728]{2,1,0:T(8,128)(2,1)S(1)} collective-permute-done((bf16[3,96,1728]{2,1,0:T(8,128)(2,1)S(1)}, bf16[3,96,1728]{2,1,0:T(8,128)(2,1)S(1)}, u32[]{:S(2)}, u32[]{:S(2)}) %collective-permute-start) | collective-permute-done | bytes 995360 | tf_op jit(solution)/shard_map/ppermute | solution.py:1594
  116.4 0.0 copy-start.4
  116.5 1.0 copy-done.4
  117.5 63.7 %middle.1 = (bf16[512,768]{1,0:T(8,128)(2,1)}, f32[512,768]{1,0:T(8,128)}, bf16[4,512,256]{2,1,0:T(8,128)(2,1)}, f32[1,768]{1,0:T(1,128)}, bf16[8,96,1216]{2,1,0...) custom-call(bf16[512,768]{1,0:T(8,128)(2,1)} %tok.5, ...), custom_call_target="tpu_custom_call" | custom-call | flops 16307453952 | bytes 25165824 | tf_op jit(solution)/shard_map/middle/pallas_call | solution.py:1088
  181.1 1.3 collective-permute-start.4
  182.4 1.3 collective-permute-start.3
  183.7 2.7 collective-permute-start.2
  186.4 0.9 collective-permute-start.1
  187.4 22.2 %attn_dq.1.d_q = bf16[2048,192]{1,0:T(8,128)(2,1)} custom-call(s32[17]{0:T(128)} %pad_add_fusion.meta, bf16[2048,256]{1,0:T(8,128)(2,1)} %get-tuple-element.71.query.q_ref.q_parts_0_, bf16[2048,256]{1,0:T(8,128)(2,1)} %bitcast.25, bf16[4096,384]{1,0:T(8,128)(2,1)} %bitcast.22, bf16[2048,384]{1,0:T(8,128)(2,1)} %get-tuple-element.82.own), custom_call_target="tpu_custom_call" | custom-call | flops 44999999488 | bytes 12582912 | tf_op jit(solution)/shard_map/attn_dq/pallas_call | solution.py:1440
  209.6 17.6 %collective-permute-done.2.got_b = bf16[2,4,96,512]{3,2,1,0:T(8,128)(2,1)S(1)} collective-permute-done((bf16[2,4,96,512]{3,2,1,0:T(8,128)(2,1)}, bf16[2,4,96,512]{3,2,1,0:T(8,128)(2,1)S(1)}, u32[]{:S(2)}, u32[]{:S(2)}) %collective-permute-start.2) | collective-permute-done | bytes 786464 | tf_op jit(solution)/shard_map/ppermute | solution.py:1605
  227.1 0.0 copy-start.2
  227.1 5.0 %collective-permute-done.1.got_a = bf16[8,96,1216]{2,1,0:T(8,128)(2,1)S(1)} collective-permute-done((bf16[8,96,1216]{2,1,0:T(8,128)(2,1)}, bf16[8,96,1216]{2,1,0:T(8,128)(2,1)S(1)}, u32[]{:S(2)}, u32[]{:S(2)}) %collective-permute-start.1) | collective-permute-done | bytes 1867808 | tf_op jit(solution)/shard_map/ppermute | solution.py:1604
  232.1 0.0 copy-start
  232.1 0.0 copy-done.2
  232.1 1.3 copy-done
  233.4 4.7 %pair_sum.1 = (bf16[4,96,1216]{2,1,0:T(8,128)(2,1)}, bf16[4,96,1216]{2,1,0:T(8,128)(2,1)}, bf16[4,96,512]{2,1,0:T(8,128)(2,1)}, bf16[4,96,512]{2,1,0:T(8,128)(2,1)}) custom-call(bf16[8,96,1216]{2,1,0:T(8,128)(2,1)} %get-tuple-element.77.ours_a, bf16[8,96,1216]{2,1,0:T(8,128)(2,1)} %copy-done, bf16[2,4,96,512]{3,2,1,0:T(8,128)(2,1)} %get-tuple-element.79.ours_b, ...), custom_call_target="tpu_custom_call" | custom-call | flops 933888 | bytes 11206656 | tf_op jit(solution)/shard_map/pair_sum/pallas_call | solution.py:1143
  238.1 1.2 collective-permute-start.6
  239.3 0.0 collective-permute-start.5
  239.3 0.0 collective-permute-done.4.do_parts_2_
  239.3 0.0 collective-permute-done.3.do_parts_1_
  239.3 49.7 %attn_dkv.1 = (bf16[2048,192]{1,0:T(8,128)(2,1)}, bf16[2048,192]{1,0:T(8,128)(2,1)}) custom-call(s32[17]{0:T(128)} %pad_add_fusion.meta, bf16[2048,384]{1,0:T(8,128)(2,1)} %get-tuple-element.82.own, bf16[2048,256]{1,0:T(8,128)(2,1)} %get-tuple-element.71.query.q_ref.q_parts_0_, bf16[4096,256]{1,0:T(8,128)(2,1)} %bitcast.28, bf16[2048,256]{1,0:T(8,128)(2,1)} %bitcast.26, ...), custom_call_target="tpu_custom_call" | custom-call | flops 60000002048 | bytes 12582912 | tf_op jit(solution)/shard_map/attn_dkv/pallas_call | solution.py:1549
  289.0 0.0 collective-permute-done.6.got_b
  289.1 0.0 copy-start.3
  289.1 0.0 collective-permute-done.5.got_a
  289.1 0.0 copy-start.1
  289.1 0.7 copy-done.3
  289.8 0.4 copy-done.1
  290.2 51.6 %tail.1 = (f32[512,768]{1,0:T(8,128)}, f32[96,192]{1,0:T(8,128)}, f32[96,192]{1,0:T(8,128)}, f32[96,96]{1,0:T(8,128)}, f32[512,384]{1,0:T(8,128)}, /*index=5*/f3...) custom-call(bf16[2048,192]{1,0:T(8,128)(2,1)} %attn_dq.1.d_q, ...), custom_call_target="tpu_custom_call" | custom-call | tf_op jit(solution)/shard_map/tail/pallas_call | solution.py:443
  341.7 4.2 %settle.1 = (bf16[512,768]{1,0:T(8,128)(2,1)}, f32[512,768]{1,0:T(8,128)}, f32[96,192]{1,0:T(8,128)}, f32[96,192]{1,0:T(8,128)}, f32[96,96]{1,0:T(8,128)}, /*ind...) custom-call(bf16[512,768]{1,0:T(8,128)(2,1)} %get-tuple-element.72.refs_0, ...), custom_call_target="tpu_custom_call" | custom-call | tf_op jit(solution)/shard_map/settle/pallas_call | solution.py:502
  345.9 1.2 slice_bitcast_fusion
Async XLA Ops:
  0.6 92.9 %copy-start.5 = (s32[16]{0:T(128)S(1)}, s32[16]{0:T(128)}, u32[]{:S(2)}) copy-start(s32[16]{0:T(128)} %param.23) | copy-start | bytes 196
  90.5 26.0 %collective-permute-start = (bf16[3,96,1728]{2,1,0:T(8,128)(2,1)S(1)}, bf16[3,96,1728]{2,1,0:T(8,128)(2,1)S(1)}, u32[]{:S(2)}, u32[]{:S(2)}) collective-permute-start(bf16[3,96,1728]{2,1,0:T(8,128)(2,1)S(1)} %dynamic-slice_bitcast_fusion), channel_id=1, source_target_pairs={{0,16},{8,24},{16,0},{24,8},{1,17},{9,25},{17,1},{25,9},{2,18},{10... | collective-permute-start | bytes 2985992 | tf_op jit(solution)/shard_map/ppermute | solution.py:1594
  116.4 1.0 copy-start.4
  181.1 58.1 %collective-permute-start.4 = (bf16[2048,256]{1,0:T(8,128)(2,1)}, bf16[2048,256]{1,0:T(8,128)(2,1)}, u32[]{:S(2)}, u32[]{:S(2)}) collective-permute-start(bf16[2048,256]{1,0:T(8,128)(2,1)} %bitcast.23), channel_id=1, source_target_pairs={{2,0},{3,1},{4,2},{5,3},{6,4},{7,5},{10,8},{11,9},{12,10},{13,11},... | collective-permute-start | bytes 3145736 | tf_op jit(solution)/shard_map/ppermute | solution.py:1608
  182.4 56.9 %collective-permute-start.3 = (bf16[2048,256]{1,0:T(8,128)(2,1)}, bf16[2048,256]{1,0:T(8,128)(2,1)}, u32[]{:S(2)}, u32[]{:S(2)}) collective-permute-start(bf16[2048,256]{1,0:T(8,128)(2,1)} %bitcast.24), channel_id=1, source_target_pairs={{1,0},{2,1},{3,2},{4,3},{5,4},{6,5},{7,6},{9,8},{10,9},{11,10},{12... | collective-permute-start | bytes 3145736 | tf_op jit(solution)/shard_map/ppermute | solution.py:1608
  183.7 43.4 %collective-permute-start.2 = (bf16[2,4,96,512]{3,2,1,0:T(8,128)(2,1)}, bf16[2,4,96,512]{3,2,1,0:T(8,128)(2,1)S(1)}, u32[]{:S(2)}, u32[]{:S(2)}) collective-permute-start(bf16[2,4,96,512]{3,2,1,0:T(8,128)(2,1)} %get-tuple-element.74), channel_id=1, source_target_pairs={{0,1},{1,0},{2,3},{3,2},{4,5},{5,4},{6,7},{7,6},{8,9},{9,8},{10,11... | collective-permute-start | bytes 2359304 | tf_op jit(solution)/shard_map/ppermute | solution.py:1605
  186.4 45.6 %collective-permute-start.1 = (bf16[8,96,1216]{2,1,0:T(8,128)(2,1)}, bf16[8,96,1216]{2,1,0:T(8,128)(2,1)S(1)}, u32[]{:S(2)}, u32[]{:S(2)}) collective-permute-start(bf16[8,96,1216]{2,1,0:T(8,128)(2,1)} %get-tuple-element.73), channel_id=1, source_target_pairs={{0,16},{8,24},{16,0},{24,8},{1,17},{9,25},{17,1},{25,9},{2,18},{10... | collective-permute-start | bytes 5603336 | tf_op jit(solution)/shard_map/ppermute | solution.py:1604
  227.1 5.0 %copy-start.2 = (bf16[2,4,96,512]{3,2,1,0:T(8,128)(2,1)}, bf16[2,4,96,512]{3,2,1,0:T(8,128)(2,1)S(1)}, u32[]{:S(2)}) copy-start(bf16[2,4,96,512]{3,2,1,0:T(8,128)(2,1)S(1)} %collective-permute-done.2.got_b) | copy-start | bytes 2359300
  232.1 1.3 copy-start
  238.1 51.0 %collective-permute-start.6 = (bf16[4,96,512]{2,1,0:T(8,128)(2,1)}, bf16[4,96,512]{2,1,0:T(8,128)(2,1)S(1)}, u32[]{:S(2)}, u32[]{:S(2)}) collective-permute-start(bf16[4,96,512]{2,1,0:T(8,128)(2,1)} %get-tuple-element.93), channel_id=1, source_target_pairs={{0,16},{8,24},{16,0},{24,8},{1,17},{9,25},{17,1},{25,9},{2,18},{10... | collective-permute-start | bytes 1179656 | tf_op jit(solution)/shard_map/ppermute | solution.py:1617
  239.3 49.8 %collective-permute-start.5 = (bf16[4,96,1216]{2,1,0:T(8,128)(2,1)}, bf16[4,96,1216]{2,1,0:T(8,128)(2,1)S(1)}, u32[]{:S(2)}, u32[]{:S(2)}) collective-permute-start(bf16[4,96,1216]{2,1,0:T(8,128)(2,1)} %get-tuple-element.91), channel_id=1, source_target_pairs={{0,1},{1,0},{2,3},{3,2},{4,5},{5,4},{6,7},{7,6},{8,9},{9,8},{10,11... | collective-permute-start | bytes 2801672 | tf_op jit(solution)/shard_map/ppermute | solution.py:1616
  289.1 0.7 copy-start.3
  289.1 1.1 copy-start.1

commit v2 on v1

--- a/solution.py
+++ b/solution.py
@@ -149,7 +149,8 @@
 def tail_kernel(
     nblk, pieces, cols, d_q, d_k, d_v, normed, w_qk, w_v, gain_m, kept_a, got_a, kept_b, got_b, tok, resid, gain,
     out_grad, out_q, out_k, out_v, out_first, out_gain, out_up, out_down, out_out,
-    grad, weights, gains, joined, weight, acc, first_got, rest_sum,
+    grad, weights, gains, joined, weight, acc,
+    tok_buf, resid_buf, normed_buf, load_sem, first_got, rest_sum,
     core_buf, side_out, side_buf, pair_buf, line_out, line_in, v_sum, v_got,
     gain_buf, gain_sum, gain_got, up_out, up_in, down_out, down_in,
     own_sem, send_s, recv_s, send_x, recv_x, send_y, recv_y, send_l, recv_l,
@@ -157,6 +158,20 @@
 ):
     head, blk = lax.axis_index("head"), lax.axis_index("blk")
     side, core, far = xor(head, 2), xor(head, 1), 3 - head
+    size = grad.shape[1]
+    turns = (far, side, core, head)
+    loads = [
+        pltpu.make_async_copy(
+            normed.at[pl.ds(pl.multiple_of(t * size, size), size)], normed_buf.at[i], load_sem.at[i]
+        )
+        for i, t in enumerate(turns)
+    ]
+    loads += [
+        pltpu.make_async_copy(tok, tok_buf, load_sem.at[4]),
+        pltpu.make_async_copy(resid, resid_buf, load_sem.at[5]),
+    ]
+    for copy in loads:
+        copy.start()
     greet(partners_of(head, blk, nblk))
     rows = grad.shape[1] // pieces
     line, place, parity = nblk // 2, lax.div(blk, 2), lax.rem(blk, 2)
@@ -238,7 +253,7 @@
     fresh = jnp.concatenate([w_v[0], w_v[1]], axis=1)
     weight[:, 2 * cols :] = jnp.where(mine, fresh, jnp.zeros_like(fresh))
     gain_row = None
-    for i, t in enumerate((far, side, core, head)):
+    for i, t in enumerate(turns):
         at = pl.ds(pl.multiple_of(t * grad.shape[1], grad.shape[1]), grad.shape[1])
         joined[:, :cols] = d_q[at, :]
         joined[:, cols : 2 * cols] = d_k[at, :]
@@ -253,7 +268,8 @@
         if i == 2:
             for p in range(pieces):
                 to_core(1, p, core).start()
-        rows_in = normed[at, :]
+        loads[i].wait()
+        rows_in = normed_buf[i]
         term = jnp.sum(whole * rows_in.astype(F32), axis=0, keepdims=True)
         gain_row = term if gain_row is None else gain_row + term
         term = dotf(rows_in, given, TN)
@@ -338,6 +354,8 @@
         def _():
             give(c, to).start()
 
+    for copy in loads[4:]:
+        copy.wait()
     for p in range(pieces):
         to_core(1, p, core).wait_recv()
         to_side(p).wait_recv()
@@ -346,8 +364,8 @@
             + part(core_buf.at[1], p)[...].astype(F32)
             + part(side_buf, p)[...].astype(F32)
         )
-        xhat, scale = statistics(part(tok, p)[...].astype(F32))
-        part(out_grad, p)[...] = part(resid, p)[...] + norm_back(norm_grad, xhat, scale, gain[...])
+        xhat, scale = statistics(part(tok_buf, p)[...].astype(F32))
+        part(out_grad, p)[...] = part(resid_buf, p)[...] + norm_back(norm_grad, xhat, scale, gain[...])
     rest_sum[...] = sum_of(place)
     for t in range(line):
 
@@ -453,11 +471,12 @@
             jax.ShapeDtypeStruct((part, inner), F32),
             jax.ShapeDtypeStruct((cols, part), F32),
         ],
-        in_specs=[WHOLE] * 14,
+        in_specs=[WHOLE] * 3 + [ANY] + [WHOLE] * 7 + [ANY] * 2 + [WHOLE],
         out_specs=[WHOLE] * 9,
         scratch_shapes=[
             vmem(4, *row), vmem(nblk, part, padded), pltpu.VMEM(gains.shape, F32),
             vmem(row[0], padded), vmem(row[1], 3 * cols), pltpu.VMEM((row[1], padded), F32),
+            vmem(*row), pltpu.VMEM(row, F32), vmem(4, *row), dma((6,)),
             vmem(2, row[0], cols), pltpu.VMEM(rest[1:], F32),
             vmem(2, *row), vmem(*row), vmem(*row),
             vmem(line, part, padded), vmem(line, part, padded),
@@ -692,12 +711,16 @@
         weight[at, 3 * pair :] = jnp.concatenate(
             [both[:, :cols], jnp.zeros((block, WIDTH - cols), BF16)], axis=1
         )
-    stores = []
-    for i, t in enumerate((head, side, core, beyond)):
-        if i == 2:
+    def make_rows(i, carry):
+        t = jnp.where(i == 0, head, jnp.where(i == 1, side, jnp.where(i == 2, core, beyond)))
+
+        @pl.when(i == 2)
+        def _():
             for k, n in order:
                 hop(ss, k, n, part(moved[k][1].at[core], n), core, core).wait_recv()
-        if i == 3:
+
+        @pl.when(i == 3)
+        def _():
             for k, n in order:
                 hop(ps, k, n, part(moved[k][1].at[beyond], n), beyond, core).wait_recv()
         total = tok.shape[0]
@@ -705,8 +728,7 @@
         xhat, _ = statistics(tok_all[t].astype(F32))
         row = (xhat * attn_gain[...]).astype(BF16)
         normed_buf[t] = row
-        stores.append(pltpu.make_async_copy(normed_buf.at[t], normed.at[at], normed_sem.at[i]))
-        stores[-1].start()
+        pltpu.make_async_copy(normed_buf.at[t], normed.at[at], normed_sem.at[i]).start()
         out = dotf(row, weight[...])
         query[at, :] = (out[:, 3 * pair :].astype(BF16).astype(F32) * size**-0.5).astype(BF16)
         done = out[:, : 3 * pair].astype(BF16)
@@ -728,6 +750,9 @@
             def _():
                 near_copy(n, slab(own, n)).start()
 
+        return carry
+
+    lax.fori_loop(0, 4, make_rows, 0)
     for o in range(nblk // 2):
 
         line.land(o)
@@ -758,8 +783,9 @@
         chunk(fs, side, b, core).wait_send()
     for b in range(nblk):
         chunk(cs, head, b, core).wait_send()
-    for copy in stores:
-        copy.wait()
+    for i in range(4):
+        at = pl.ds(0, tok.shape[0])
+        pltpu.make_async_copy(normed_buf.at[i], normed.at[at], normed_sem.at[i]).wait()
     for n in range(pieces):
 
         @pl.when((blk >= 2) | (odd == 1))
@@ -856,7 +882,7 @@
     out, grad_resid, grad_wide, gain_part, keep_a, give_a, keep_b, give_b, query_later,
     up, down, w_out, up_grad, down_grad, out_grad, mixed, wide_parts, up_got, down_got, out_got,
     sems, out_sems, send_m, recv_m, send_g, recv_g, send_c, recv_c,
-    send_z, recv_z, send_y, recv_y, hidden_all, pre_all, normed_t, cot_t, late_far, send_l, recv_l,
+    send_z, recv_z, send_y, recv_y, hidden_all, pre_all, normed_t, cot_t, total, grad_normed, normed_rows, branch_rows, branch_t, late_far, send_l, recv_l,
 ):
     head, blk = lax.axis_index("head"), lax.axis_index("blk")
     x, core_index = lax.div(head, 2), lax.rem(head, 2)
@@ -958,26 +984,43 @@
     xhat, scale = statistics(resid)
     normed = (xhat * gain[...]).astype(BF16)
     cotangent = cot[...]
-    total, grad_normed = resid, None
+    total[...] = resid
+    grad_normed[...] = jnp.zeros_like(resid)
+
+    def chunk_of(i):
+        far = jnp.where(i < 2, 1 - x, x)
+        return 2 * far + jnp.where(lax.rem(i, 2) == 0, 1 - core_index, core_index)
 
     def to_core(n, k):
         mine, theirs = ((up_grad, up_got), (down_grad, down_got), (out_grad, out_got))[k]
         return remote(mine.at[2 * n], theirs.at[n], send_c.at[k, n], recv_c.at[k, n], core, blk)
 
+    normed_rows[...] = normed
     normed_t[...] = normed.T
     cot_t[...] = cotangent.T
-    for n, i in enumerate(turns):
-        for copy in load(i, 1) + load(i, 2):
-            copy.wait()
-        hidden, slope = gelu_both(dotf(normed, up[i]))
+    def arrived(which, i):
+        target = (w_out, up, down)[which].at[i, pl.ds(0, part)]
+        for b in range(nblk):
+            pltpu.make_async_copy(target, target, sems.at[which, i, b]).wait()
+
+    def forward(n, carry):
+        i = jnp.where(n < 2, n + 2, 3 - n)
+        arrived(1, i)
+        arrived(2, i)
+        hidden, slope = gelu_both(dotf(normed_rows[...], up[i]))
         hidden_all[i] = hidden.astype(BF16)
-        pre_all[i] = (slope * dotf(cotangent, down[i])).astype(BF16)
-        total = total + dotf(hidden_all[i], down[i], NT)
-        term = dotf(pre_all[i], up[i], NT)
-        grad_normed = term if grad_normed is None else grad_normed + term
-        for p in range(n * pieces // heads_of, (n + 1) * pieces // heads_of):
-            relay(p)
-    grad = cotangent.astype(F32) + norm_back(grad_normed, xhat, scale, gain[...])
+        pre_all[i] = (slope * dotf(cot[...], down[i])).astype(BF16)
+        total[...] += dotf(hidden_all[i], down[i], NT)
+        grad_normed[...] += dotf(pre_all[i], up[i], NT)
+
+        @pl.loop(0, pieces // heads_of)
+        def _(p):
+            relay(n * (pieces // heads_of) + p)
+
+        return carry
+
+    lax.fori_loop(0, heads_of, forward, 0)
+    grad = cotangent.astype(F32) + norm_back(grad_normed[...], xhat, scale, gain[...])
     branch_grad = grad.astype(BF16)
     lane = lax.broadcasted_iota(jnp.int32, (tok.shape[0], WIDTH), 1)
 
@@ -986,9 +1029,11 @@
             wide_parts.at[to], grad_wide.at[slot], send_g.at[i], recv_g.at[i], to, blk
         )
 
-    for i in range(heads_of):
-        h = chunks[i]
-        rows = dotf(branch_grad, w_out[i]).astype(BF16).astype(F32)
+    branch_rows[...] = branch_grad
+
+    def widen(i, carry):
+        h = chunk_of(i)
+        rows = dotf(branch_rows[...], w_out[i]).astype(BF16).astype(F32)
         product = rows * mixed[h].astype(F32)
         wide = jnp.concatenate([rows, jnp.zeros((rows.shape[0], WIDTH - cols), F32)], axis=1)
         for k in range(heads):
@@ -998,23 +1043,33 @@
             for c, piece in enumerate(split_parts(-delta)):
                 wide = jnp.where(lane == cols + SPLITS * k + c, piece, wide)
         wide_parts[h] = wide.astype(BF16)
-        if i < 3:
+
+        @pl.when(i < 3)
+        def _():
             wide_copy(i, h, head).start()
+
+        return carry
+
+    lax.fori_loop(0, heads_of, widen, 0)
     grad_wide[head] = wide_parts[head]
-    out[...] = total.astype(BF16)
-    gain_part[...] = jnp.sum(grad_normed * xhat, axis=0, keepdims=True)
+    out[...] = total[...].astype(BF16)
+    gain_part[...] = jnp.sum(grad_normed[...] * xhat, axis=0, keepdims=True)
     grad_resid[...] = grad
-    for i in range(heads_of):
+    branch_t[...] = branch_grad.T
+
+    def weigh(i, carry):
         up_grad[i] = dotf(normed_t[...], pre_all[i]).astype(BF16)
         down_grad[i] = dotf(cot_t[...], hidden_all[i]).astype(BF16)
-        if i % 2 == 0:
-            to_core(i // 2, 0).start()
-            to_core(i // 2, 1).start()
-    branch_t = branch_grad.T
-    for i in range(heads_of):
-        out_grad[i] = dotf(branch_t, mixed[chunks[i]]).astype(BF16)
-        if i % 2 == 0:
-            to_core(i // 2, 2).start()
+        out_grad[i] = dotf(branch_t[...], mixed[chunk_of(i)]).astype(BF16)
+
+        @pl.when(lax.rem(i, 2) == 0)
+        def _():
+            for k in range(3):
+                to_core(lax.div(i, 2), k).start()
+
+        return carry
+
+    lax.fori_loop(0, heads_of, weigh, 0)
 
     def store(k, source, target, lo):
         size = source.shape[1]
@@ -1112,6 +1167,8 @@
             dma((pieces,)), dma((pieces,)), dma((pieces,)), dma((pieces,)),
             vmem(heads_of, rows, up_cols), vmem(heads_of, rows, up_cols),
             vmem(width, rows), vmem(width, rows),
+            pltpu.VMEM((rows, width), F32), pltpu.VMEM((rows, width), F32),
+            vmem(rows, width), vmem(rows, width), vmem(width, rows),
             vmem(*late.shape), dma, dma,
         ],
         compiler_params=pltpu.CompilerParams(
@@ -1185,14 +1242,14 @@
     def step(j,c):
         cum,best=c
         return cum+meta[1+j],jnp.where(cum<=t,cum,best)
-    return lax.fori_loop(0,ndocs,step,(jnp.int32(0),jnp.zeros(t.shape,jnp.int32)),unroll=True)[1]
+    return lax.fori_loop(0,ndocs,step,(jnp.int32(0),jnp.zeros(t.shape,jnp.int32)))[1]
 
 def ends_vec(meta, ndocs, t):
     def step(j,c):
         cum,best=c
         ln=meta[1+j]
         return cum+ln,jnp.where(cum<=t,cum+ln,best)
-    return lax.fori_loop(0,ndocs,step,(jnp.int32(0),jnp.zeros(t.shape,jnp.int32)),unroll=True)[1]
+    return lax.fori_loop(0,ndocs,step,(jnp.int32(0),jnp.zeros(t.shape,jnp.int32)))[1]
 
 def widened(columns, heads):
     rows, width = columns.shape
@@ -1248,10 +1305,20 @@
     lax.fori_loop(start, chunks, build, 0)
 
 
-def three(lo,a,b,hi,body):
-    lax.fori_loop(lo,a,lambda j,_: body(j,True),None)
-    lax.fori_loop(a,b,lambda j,_: body(j,False),None)
-    lax.fori_loop(b,hi,lambda j,_: body(j,True),None)
+def three(lo, a, b, hi, body):
+    edge = a - lo
+
+    def masked(n, carry):
+        body(jnp.where(n < edge, lo + n, b + n - edge), True)
+        return carry
+
+    def free(n, carry):
+        body(n, False)
+        return carry
+
+    lax.fori_loop(0, edge + hi - b, masked, 0)
+    lax.fori_loop(a, b, free, 0)
+
 
 def query_tiles(meta, ndocs, t0, wbase, tq, tk):
     lo = (doc_start(meta, ndocs, t0) - wbase) // tk
@@ -1302,8 +1369,9 @@
         k = k_ref[pl.ds(off, tk), :]
         if masked:
             vis = visible(off)
+        scores = [dotf(k, qt[h]) for h in range(heads)]
         for h in range(heads):
-            p = jnp.exp(dotf(k, qt[h]))
+            p = jnp.exp(scores[h])
             if masked:
                 p = jnp.where(vis, p, 0.0)
             acc_ref[h] += dotf(vt_ref[h, :, pl.ds(off, tk)], p.astype(BF16))
@@ -1420,11 +1488,12 @@
         if masked:
             u = wbase + off + lax.broadcasted_iota(jnp.int32, (tk, tq), 0)
             vis = (u >= srow) & (u <= trow)
+        made = [(dotf(k, qt[h]), dotf(v, dot[h])) for h in range(heads)]
         for h in range(heads):
-            p = jnp.exp(dotf(k, qt[h]))
+            p = jnp.exp(made[h][0])
             if masked:
                 p = jnp.where(vis, p, 0.0)
-            ds = (p * dotf(v, dot[h])).astype(BF16)
+            ds = (p * made[h][1]).astype(BF16)
             acc_ref[h] += dotf(kt_ref[h, :, pl.ds(off, tk)], ds)
 
     three(*query_tiles(meta, ndocs, t0, wbase, tq, tk), body)
@@ -1593,7 +1662,7 @@
     mine = lax.dynamic_index_in_dim(gathered, lax.axis_index("head"), 0, keepdims=False)[early:]
     late = lax.ppermute(mine, "head", beside)
     mixed_parts, query_wide = attention_fwd(
-        meta, query, earlier, own, heads, rows, 2 * rows
+        meta, query, earlier, own, heads, rows, rows
     )
     late, mixed_parts = lax.optimization_barrier((late, mixed_parts))
     layer_output, grad_resid, grad_parts, gain_mlp_part, keep_a, give_a, keep_b, give_b, query_later = middle(
@@ -1609,7 +1678,7 @@
     ]
     queries_later = [query_wide, query_later.reshape(2 * block, WIDTH)]
     grad_query = attention_dq(
-        meta, query_wide, grad_wide, earlier, own, heads, rows, 2 * rows
+        meta, query_wide, grad_wide, earlier, own, heads, rows, rows
     )
     got_a, got_b, grad_query = lax.optimization_barrier((got_a, got_b, grad_query))
     keep_a, give_a, keep_b, give_b = pair_sum(keep_a, got_a, keep_b, got_b)

time: 347 us -> 347 us (level); the launches traced: 348 us -> 352 us
  waiting for transfers between devices: 27.8 us -> 36.1 us
    pallas_call x1, Pallas kernels: 51.6 us -> 66.9 us  [tail(): pl.pallas_call(functools.partial(tail_kernel, nblk, pieces, cols), out_sh...]
    pallas_call x1, Pallas kernels: 49.7 us -> 41.3 us  [attention_dkv(): pl.pallas_call(functools.partial(dkv_kernel, heads, ndocs, tq, tk), grid=...]
    ppermute x1, waiting for transfers between devices: 17.6 us -> 23.8 us  [on_device(): got_b = lax.ppermute(give_b, 'blk', across)]
    pallas_call x1, Pallas kernels: 22.2 us -> 16.8 us  [attention_dq(): pl.pallas_call(functools.partial(dq_kernel, heads, ndocs, tq, tk), grid=(...]
  transfers between devices with their start and end apart: 7 -> 7, of which waited for: 3 -> 3; matrix products, arithmetic and copies ran while one was open for 0% -> 0% of each run, Pallas kernels for 27% -> 22%
where the time goes in v2:
time: 347 us; the launch traced here: 352 us
  Pallas kernels  300 us (86%)
  waiting for transfers between devices  36.1 us (10%)
  starting transfers between devices  9.12 us (3%)
  local copies, waits for them, and re-layouts  5.88 us (2%)
    pallas_call x1, Pallas kernels, front(): pl.pallas_call(functools.partial(front_kernel, nblk, parts, pieces, early...  88 us
    pallas_call x1, Pallas kernels, tail(): pl.pallas_call(functools.partial(tail_kernel, nblk, pieces, cols), out_sh...  66.9 us
    pallas_call x1, Pallas kernels, middle(): pl.pallas_call(functools.partial(middle_kernel, nblk, up_cols, cut, piece...  63.8 us
    pallas_call x1, Pallas kernels, attention_dkv(): pl.pallas_call(functools.partial(dkv_kernel, heads, ndocs, tq, tk), grid=...  41.3 us
    ppermute x1, waiting for transfers between devices, on_device(): got_b = lax.ppermute(give_b, 'blk', across)  23.8 us
    pallas_call x1, Pallas kernels, attention_dq(): pl.pallas_call(functools.partial(dq_kernel, heads, ndocs, tq, tk), grid=(...  16.8 us
    pallas_call x1, Pallas kernels, attention_fwd(): pl.pallas_call(functools.partial(fwd_kernel, heads, ndocs, tq, tk), grid=...  14 us
    ppermute x1, waiting for transfers between devices, on_device(): late = lax.ppermute(mine, 'head', beside)  7.93 us
  transfers between devices with their start and end apart: 7, of which 3 were waited for; matrix products, arithmetic and copies ran while one was open for 0% of the time, Pallas kernels for 22%

profile of v2, /device:TPU:0, one launch (start us, length us, event | category | flops | bytes accessed | tf_op | source)
XLA Modules:
  0.0 352.2 jit_solution(10603419089430186017)
XLA Ops:
  0.6 0.0 copy-start.5
  0.7 88.0 %front.1 = (bf16[2048,768]{1,0:T(8,128)(2,1)}, bf16[2048,256]{1,0:T(8,128)(2,1)}, bf16[2048,384]{1,0:T(8,128)(2,1)}, bf16[2,2048,384]{2,1,0:T(8,128)(2,1)}, bf16...) custom-call(bf16[512,768]{1,0:T(8,128)(2,1)} %tok.5, ...), custom_call_target="tpu_custom_call" | custom-call | tf_op jit(solution)/shard_map/front/pallas_call | solution.py:831
  88.7 1.3 dynamic-slice_bitcast_fusion
  90.0 3.1 collective-permute-start
  93.1 0.0 copy-done.5
  93.1 0.6 pad_add_fusion.meta
  93.7 14.0 %attn_fwd.1 = (bf16[4,512,192]{2,1,0:T(8,128)(2,1)}, bf16[2048,256]{1,0:T(8,128)(2,1)}) custom-call(s32[17]{0:T(128)} %pad_add_fusion.meta, bf16[2048,256]{1,0:T(8,128)(2,1)} %get-tuple-element.64.q_ref, bf16[4096,384]{1,0:T(8,128)(2,1)} %bitcast.21, bf16[2048,384]{1,0:T(8,128)(2,1)} %get-tuple-element.82.own), custom_call_target="tpu_custom_call" | custom-call | flops 30000001024 | bytes 12582912 | tf_op jit(solution)/shard_map/attn_fwd/pallas_call | solution.py:1431
  107.8 7.9 %collective-permute-done.late = bf16[3,96,1728]{2,1,0:T(8,128)(2,1)S(1)} collective-permute-done((bf16[3,96,1728]{2,1,0:T(8,128)(2,1)S(1)}, bf16[3,96,1728]{2,1,0:T(8,128)(2,1)S(1)}, u32[]{:S(2)}, u32[]{:S(2)}) %collective-permute-start) | collective-permute-done | bytes 995360 | tf_op jit(solution)/shard_map/ppermute | solution.py:1663
  115.7 0.0 copy-start.4
  115.7 1.0 copy-done.4
  116.7 63.8 %middle.1 = (bf16[512,768]{1,0:T(8,128)(2,1)}, f32[512,768]{1,0:T(8,128)}, bf16[4,512,256]{2,1,0:T(8,128)(2,1)}, f32[1,768]{1,0:T(1,128)}, bf16[8,96,1216]{2,1,0...) custom-call(bf16[512,768]{1,0:T(8,128)(2,1)} %tok.5, ...), custom_call_target="tpu_custom_call" | custom-call | flops 16307453952 | bytes 25165824 | tf_op jit(solution)/shard_map/middle/pallas_call | solution.py:1143
  180.5 1.3 collective-permute-start.4
  181.8 1.3 collective-permute-start.3
  183.1 2.7 collective-permute-start.2
  185.8 0.0 collective-permute-start.1
  185.8 16.8 %attn_dq.1.d_q = bf16[2048,192]{1,0:T(8,128)(2,1)} custom-call(s32[17]{0:T(128)} %pad_add_fusion.meta, bf16[2048,256]{1,0:T(8,128)(2,1)} %get-tuple-element.71.query.q_ref.q_parts_0_, bf16[2048,256]{1,0:T(8,128)(2,1)} %bitcast.25, bf16[4096,384]{1,0:T(8,128)(2,1)} %bitcast.22, bf16[2048,384]{1,0:T(8,128)(2,1)} %get-tuple-element.82.own), custom_call_target="tpu_custom_call" | custom-call | flops 44999999488 | bytes 12582912 | tf_op jit(solution)/shard_map/attn_dq/pallas_call | solution.py:1509
  202.6 23.8 %collective-permute-done.2.got_b = bf16[2,4,96,512]{3,2,1,0:T(8,128)(2,1)S(1)} collective-permute-done((bf16[2,4,96,512]{3,2,1,0:T(8,128)(2,1)}, bf16[2,4,96,512]{3,2,1,0:T(8,128)(2,1)S(1)}, u32[]{:S(2)}, u32[]{:S(2)}) %collective-permute-start.2) | collective-permute-done | bytes 786464 | tf_op jit(solution)/shard_map/ppermute | solution.py:1674
  226.4 0.0 copy-start.2
  226.4 4.4 %collective-permute-done.1.got_a = bf16[8,96,1216]{2,1,0:T(8,128)(2,1)S(1)} collective-permute-done((bf16[8,96,1216]{2,1,0:T(8,128)(2,1)}, bf16[8,96,1216]{2,1,0:T(8,128)(2,1)S(1)}, u32[]{:S(2)}, u32[]{:S(2)}) %collective-permute-start.1) | collective-permute-done | bytes 1867808 | tf_op jit(solution)/shard_map/ppermute | solution.py:1673
  230.8 0.0 copy-start
  230.8 0.0 copy-done.2
  230.8 1.3 copy-done
  232.1 4.7 %pair_sum.1 = (bf16[4,96,1216]{2,1,0:T(8,128)(2,1)}, bf16[4,96,1216]{2,1,0:T(8,128)(2,1)}, bf16[4,96,512]{2,1,0:T(8,128)(2,1)}, bf16[4,96,512]{2,1,0:T(8,128)(2,1)}) custom-call(bf16[8,96,1216]{2,1,0:T(8,128)(2,1)} %get-tuple-element.77.ours_a, bf16[8,96,1216]{2,1,0:T(8,128)(2,1)} %copy-done, bf16[2,4,96,512]{3,2,1,0:T(8,128)(2,1)} %get-tuple-element.79.ours_b, ...), custom_call_target="tpu_custom_call" | custom-call | flops 933888 | bytes 11206656 | tf_op jit(solution)/shard_map/pair_sum/pallas_call | solution.py:1200
  236.7 0.3 collective-permute-start.6
  237.0 0.4 collective-permute-start.5
  237.4 0.0 collective-permute-done.4.do_parts_2_
  237.4 0.0 collective-permute-done.3.do_parts_1_
  237.4 41.3 %attn_dkv.1 = (bf16[2048,192]{1,0:T(8,128)(2,1)}, bf16[2048,192]{1,0:T(8,128)(2,1)}) custom-call(s32[17]{0:T(128)} %pad_add_fusion.meta, bf16[2048,384]{1,0:T(8,128)(2,1)} %get-tuple-element.82.own, bf16[2048,256]{1,0:T(8,128)(2,1)} %get-tuple-element.71.query.q_ref.q_parts_0_, bf16[4096,256]{1,0:T(8,128)(2,1)} %bitcast.28, bf16[2048,256]{1,0:T(8,128)(2,1)} %bitcast.26, ...), custom_call_target="tpu_custom_call" | custom-call | flops 60000002048 | bytes 12582912 | tf_op jit(solution)/shard_map/attn_dkv/pallas_call | solution.py:1618
  278.8 0.0 collective-permute-done.6.got_b
  278.8 0.0 copy-start.3
  278.8 0.0 collective-permute-done.5.got_a
  278.8 0.0 copy-start.1
  278.8 0.7 copy-done.3
  279.5 0.4 copy-done.1
  279.9 66.9 %tail.1 = (f32[512,768]{1,0:T(8,128)}, f32[96,192]{1,0:T(8,128)}, f32[96,192]{1,0:T(8,128)}, f32[96,96]{1,0:T(8,128)}, f32[512,384]{1,0:T(8,128)}, /*index=5*/f3...) custom-call(bf16[2048,192]{1,0:T(8,128)(2,1)} %attn_dq.1.d_q, ...), custom_call_target="tpu_custom_call" | custom-call | tf_op jit(solution)/shard_map/tail/pallas_call | solution.py:461
  346.8 4.2 %settle.1 = (bf16[512,768]{1,0:T(8,128)(2,1)}, f32[512,768]{1,0:T(8,128)}, f32[96,192]{1,0:T(8,128)}, f32[96,192]{1,0:T(8,128)}, f32[96,96]{1,0:T(8,128)}, /*ind...) custom-call(bf16[512,768]{1,0:T(8,128)(2,1)} %get-tuple-element.72.refs_0, ...), custom_call_target="tpu_custom_call" | custom-call | tf_op jit(solution)/shard_map/settle/pallas_call | solution.py:521
  351.0 1.2 slice_bitcast_fusion
Async XLA Ops:
  0.6 92.5 %copy-start.5 = (s32[16]{0:T(128)S(1)}, s32[16]{0:T(128)}, u32[]{:S(2)}) copy-start(s32[16]{0:T(128)} %param.23) | copy-start | bytes 196
  90.0 25.7 %collective-permute-start = (bf16[3,96,1728]{2,1,0:T(8,128)(2,1)S(1)}, bf16[3,96,1728]{2,1,0:T(8,128)(2,1)S(1)}, u32[]{:S(2)}, u32[]{:S(2)}) collective-permute-start(bf16[3,96,1728]{2,1,0:T(8,128)(2,1)S(1)} %dynamic-slice_bitcast_fusion), channel_id=1, source_target_pairs={{0,16},{8,24},{16,0},{24,8},{1,17},{9,25},{17,1},{25,9},{2,18},{10... | collective-permute-start | bytes 2985992 | tf_op jit(solution)/shard_map/ppermute | solution.py:1663
  115.7 1.0 copy-start.4
  180.5 56.9 %collective-permute-start.4 = (bf16[2048,256]{1,0:T(8,128)(2,1)}, bf16[2048,256]{1,0:T(8,128)(2,1)}, u32[]{:S(2)}, u32[]{:S(2)}) collective-permute-start(bf16[2048,256]{1,0:T(8,128)(2,1)} %bitcast.23), channel_id=1, source_target_pairs={{2,0},{3,1},{4,2},{5,3},{6,4},{7,5},{10,8},{11,9},{12,10},{13,11},... | collective-permute-start | bytes 3145736 | tf_op jit(solution)/shard_map/ppermute | solution.py:1677
  181.8 55.6 %collective-permute-start.3 = (bf16[2048,256]{1,0:T(8,128)(2,1)}, bf16[2048,256]{1,0:T(8,128)(2,1)}, u32[]{:S(2)}, u32[]{:S(2)}) collective-permute-start(bf16[2048,256]{1,0:T(8,128)(2,1)} %bitcast.24), channel_id=1, source_target_pairs={{1,0},{2,1},{3,2},{4,3},{5,4},{6,5},{7,6},{9,8},{10,9},{11,10},{12... | collective-permute-start | bytes 3145736 | tf_op jit(solution)/shard_map/ppermute | solution.py:1677
  183.1 43.3 %collective-permute-start.2 = (bf16[2,4,96,512]{3,2,1,0:T(8,128)(2,1)}, bf16[2,4,96,512]{3,2,1,0:T(8,128)(2,1)S(1)}, u32[]{:S(2)}, u32[]{:S(2)}) collective-permute-start(bf16[2,4,96,512]{3,2,1,0:T(8,128)(2,1)} %get-tuple-element.74), channel_id=1, source_target_pairs={{0,1},{1,0},{2,3},{3,2},{4,5},{5,4},{6,7},{7,6},{8,9},{9,8},{10,11... | collective-permute-start | bytes 2359304 | tf_op jit(solution)/shard_map/ppermute | solution.py:1674
  185.8 45.0 %collective-permute-start.1 = (bf16[8,96,1216]{2,1,0:T(8,128)(2,1)}, bf16[8,96,1216]{2,1,0:T(8,128)(2,1)S(1)}, u32[]{:S(2)}, u32[]{:S(2)}) collective-permute-start(bf16[8,96,1216]{2,1,0:T(8,128)(2,1)} %get-tuple-element.73), channel_id=1, source_target_pairs={{0,16},{8,24},{16,0},{24,8},{1,17},{9,25},{17,1},{25,9},{2,18},{10... | collective-permute-start | bytes 5603336 | tf_op jit(solution)/shard_map/ppermute | solution.py:1673
  226.4 4.4 %copy-start.2 = (bf16[2,4,96,512]{3,2,1,0:T(8,128)(2,1)}, bf16[2,4,96,512]{3,2,1,0:T(8,128)(2,1)S(1)}, u32[]{:S(2)}) copy-start(bf16[2,4,96,512]{3,2,1,0:T(8,128)(2,1)S(1)} %collective-permute-done.2.got_b) | copy-start | bytes 2359300
  230.8 1.3 copy-start
  236.7 42.0 %collective-permute-start.6 = (bf16[4,96,512]{2,1,0:T(8,128)(2,1)}, bf16[4,96,512]{2,1,0:T(8,128)(2,1)S(1)}, u32[]{:S(2)}, u32[]{:S(2)}) collective-permute-start(bf16[4,96,512]{2,1,0:T(8,128)(2,1)} %get-tuple-element.93), channel_id=1, source_target_pairs={{0,16},{8,24},{16,0},{24,8},{1,17},{9,25},{17,1},{25,9},{2,18},{10... | collective-permute-start | bytes 1179656 | tf_op jit(solution)/shard_map/ppermute | solution.py:1686
  237.0 41.7 %collective-permute-start.5 = (bf16[4,96,1216]{2,1,0:T(8,128)(2,1)}, bf16[4,96,1216]{2,1,0:T(8,128)(2,1)S(1)}, u32[]{:S(2)}, u32[]{:S(2)}) collective-permute-start(bf16[4,96,1216]{2,1,0:T(8,128)(2,1)} %get-tuple-element.91), channel_id=1, source_target_pairs={{0,1},{1,0},{2,3},{3,2},{4,5},{5,4},{6,7},{7,6},{8,9},{9,8},{10,11... | collective-permute-start | bytes 2801672 | tf_op jit(solution)/shard_map/ppermute | solution.py:1685
  278.8 0.7 copy-start.3
  278.8 1.1 copy-start.1

commit v3 on v2

--- a/solution.py
+++ b/solution.py
@@ -148,7 +148,7 @@
 
 def tail_kernel(
     nblk, pieces, cols, d_q, d_k, d_v, normed, w_qk, w_v, gain_m, kept_a, got_a, kept_b, got_b, tok, resid, gain,
-    out_grad, out_q, out_k, out_v, out_first, out_gain, out_up, out_down, out_out,
+    out_grad, out_q, out_k, out_v, out_first, out_gain_a, out_gain_m, out_up, out_down, out_out,
     grad, weights, gains, joined, weight, acc,
     tok_buf, resid_buf, normed_buf, load_sem, first_got, rest_sum,
     core_buf, side_out, side_buf, pair_buf, line_out, line_in, v_sum, v_got,
@@ -387,7 +387,9 @@
     out_out[...] = rest_sum[:, 2 * inner :].T
     for i, to in enumerate(peers):
         gain_copy(i, to).wait_recv()
-    out_gain[...] = gain_sum[...] + gain_got[0] + gain_got[1] + gain_got[2]
+    gain_total = gain_sum[...] + gain_got[0] + gain_got[1] + gain_got[2]
+    out_gain_a[...] = gain_total[0]
+    out_gain_m[...] = gain_total[1]
 
     @pl.when(head == 0)
     def _():
@@ -466,13 +468,14 @@
             jax.ShapeDtypeStruct((part, cols), F32),
             jax.ShapeDtypeStruct(half, F32),
             jax.ShapeDtypeStruct((row[0], 2 * cols), F32),
-            jax.ShapeDtypeStruct(gains.shape[1:], F32),
+            jax.ShapeDtypeStruct((1, part), F32),
+            jax.ShapeDtypeStruct((1, part), F32),
             jax.ShapeDtypeStruct((part, inner), F32),
             jax.ShapeDtypeStruct((part, inner), F32),
             jax.ShapeDtypeStruct((cols, part), F32),
         ],
         in_specs=[WHOLE] * 3 + [ANY] + [WHOLE] * 7 + [ANY] * 2 + [WHOLE],
-        out_specs=[WHOLE] * 9,
+        out_specs=[WHOLE] * 10,
         scratch_shapes=[
             vmem(4, *row), vmem(nblk, part, padded), pltpu.VMEM(gains.shape, F32),
             vmem(row[0], padded), vmem(row[1], 3 * cols), pltpu.VMEM((row[1], padded), F32),
@@ -1693,7 +1696,7 @@
         keep_a, got_a, keep_b, got_b, tokens, grad_resid, attn_gain,
     )
     (
-        layer_output, grad_tokens, final_query, final_key, final_value, grad_first, gain_sums,
+        layer_output, grad_tokens, final_query, final_key, final_value, grad_first, final_a, final_m,
         final_up, final_down, final_out,
     ) = settle([layer_output] + list(outs))
     return (
@@ -1706,8 +1709,8 @@
         final_out,
         final_up,
         final_down.T,
-        gain_sums[0].reshape(part),
-        gain_sums[1].reshape(part),
+        final_a.reshape(part),
+        final_m.reshape(part),
     )
 
 

time: 347 us -> 346 us (level); the launches traced: 352 us -> 342 us
  Pallas kernels: 300 us -> 289 us
  starting transfers between devices: 9.12 us -> 13.8 us
  waiting for transfers between devices: 36.1 us -> 32.4 us
    pallas_call x1, Pallas kernels: 41.3 us -> 29.2 us  [attention_dkv(): pl.pallas_call(functools.partial(dkv_kernel, heads, ndocs, tq, tk), grid=...]
    ppermute x1, waiting for transfers between devices: 23.8 us -> 18.7 us  [on_device(): got_b = lax.ppermute(give_b, 'blk', across)]
    pallas_call x1, Pallas kernels: 63.8 us -> 59.2 us  [middle(): pl.pallas_call(functools.partial(middle_kernel, nblk, up_cols, cut, piece...]
    pallas_call x1, Pallas kernels: 66.9 us -> 71.1 us  [tail(): pl.pallas_call(functools.partial(tail_kernel, nblk, pieces, cols), out_sh...]
  transfers between devices with their start and end apart: 7 -> 7, of which waited for: 3 -> 3; matrix products, arithmetic and copies ran while one was open for 0% -> 0% of each run, Pallas kernels for 22% -> 20%
where the time goes in v3:
time: 346 us; the launch traced here: 342 us
  Pallas kernels  289 us (84%)
  waiting for transfers between devices  32.4 us (9%)
  starting transfers between devices  13.8 us (4%)
  local copies, waits for them, and re-layouts  4.66 us (1%)
    pallas_call x1, Pallas kernels, front(): pl.pallas_call(functools.partial(front_kernel, nblk, parts, pieces, early...  88 us
    pallas_call x1, Pallas kernels, tail(): pl.pallas_call(functools.partial(tail_kernel, nblk, pieces, cols), out_sh...  71.1 us
    pallas_call x1, Pallas kernels, middle(): pl.pallas_call(functools.partial(middle_kernel, nblk, up_cols, cut, piece...  59.2 us
    pallas_call x1, Pallas kernels, attention_dkv(): pl.pallas_call(functools.partial(dkv_kernel, heads, ndocs, tq, tk), grid=...  29.2 us
    ppermute x1, waiting for transfers between devices, on_device(): got_b = lax.ppermute(give_b, 'blk', across)  18.7 us
    pallas_call x1, Pallas kernels, attention_dq(): pl.pallas_call(functools.partial(dq_kernel, heads, ndocs, tq, tk), grid=(...  18.1 us
    pallas_call x1, Pallas kernels, attention_fwd(): pl.pallas_call(functools.partial(fwd_kernel, heads, ndocs, tq, tk), grid=...  14.9 us
    ppermute x1, waiting for transfers between devices, on_device(): late = lax.ppermute(mine, 'head', beside)  7.1 us
  transfers between devices with their start and end apart: 7, of which 3 were waited for; matrix products, arithmetic and copies ran while one was open for 0% of the time, Pallas kernels for 20%

profile of v3, /device:TPU:0, one launch (start us, length us, event | category | flops | bytes accessed | tf_op | source)
XLA Modules:
  0.0 341.7 jit_solution(1536118623286431687)
XLA Ops:
  0.6 0.0 copy-start.5
  0.7 88.0 %front.1 = (bf16[2048,768]{1,0:T(8,128)(2,1)}, bf16[2048,256]{1,0:T(8,128)(2,1)}, bf16[2048,384]{1,0:T(8,128)(2,1)}, bf16[2,2048,384]{2,1,0:T(8,128)(2,1)}, bf16...) custom-call(bf16[512,768]{1,0:T(8,128)(2,1)} %tok.5, ...), custom_call_target="tpu_custom_call" | custom-call | tf_op jit(solution)/shard_map/front/pallas_call | solution.py:834
  88.7 1.3 dynamic-slice_bitcast_fusion
  90.0 3.1 collective-permute-start
  93.1 0.0 copy-done.5
  93.1 0.6 pad_add_fusion.meta
  93.7 14.9 %attn_fwd.1 = (bf16[4,512,192]{2,1,0:T(8,128)(2,1)}, bf16[2048,256]{1,0:T(8,128)(2,1)}) custom-call(s32[17]{0:T(128)} %pad_add_fusion.meta, bf16[2048,256]{1,0:T(8,128)(2,1)} %get-tuple-element.66.q_ref, bf16[4096,384]{1,0:T(8,128)(2,1)} %bitcast.19, bf16[2048,384]{1,0:T(8,128)(2,1)} %get-tuple-element.84.own), custom_call_target="tpu_custom_call" | custom-call | flops 30000001024 | bytes 12582912 | tf_op jit(solution)/shard_map/attn_fwd/pallas_call | solution.py:1434
  108.6 7.1 %collective-permute-done.late = bf16[3,96,1728]{2,1,0:T(8,128)(2,1)S(1)} collective-permute-done((bf16[3,96,1728]{2,1,0:T(8,128)(2,1)S(1)}, bf16[3,96,1728]{2,1,0:T(8,128)(2,1)S(1)}, u32[]{:S(2)}, u32[]{:S(2)}) %collective-permute-start) | collective-permute-done | bytes 995360 | tf_op jit(solution)/shard_map/ppermute | solution.py:1666
  115.7 0.0 copy-start.4
  115.7 1.0 copy-done.4
  116.7 59.2 %middle.1 = (bf16[512,768]{1,0:T(8,128)(2,1)}, f32[512,768]{1,0:T(8,128)}, bf16[4,512,256]{2,1,0:T(8,128)(2,1)}, f32[1,768]{1,0:T(1,128)}, bf16[8,96,1216]{2,1,0...) custom-call(bf16[512,768]{1,0:T(8,128)(2,1)} %tok.5, ...), custom_call_target="tpu_custom_call" | custom-call | flops 16307453952 | bytes 25165824 | tf_op jit(solution)/shard_map/middle/pallas_call | solution.py:1146
  176.0 1.3 collective-permute-start.4
  177.3 1.3 collective-permute-start.3
  178.6 2.7 collective-permute-start.2
  181.3 3.3 collective-permute-start.1
  184.5 18.1 %attn_dq.1.d_q = bf16[2048,192]{1,0:T(8,128)(2,1)} custom-call(s32[17]{0:T(128)} %pad_add_fusion.meta, bf16[2048,256]{1,0:T(8,128)(2,1)} %get-tuple-element.73.query.q_ref.q_parts_0_, bf16[2048,256]{1,0:T(8,128)(2,1)} %bitcast.23, bf16[4096,384]{1,0:T(8,128)(2,1)} %bitcast.20, bf16[2048,384]{1,0:T(8,128)(2,1)} %get-tuple-element.84.own), custom_call_target="tpu_custom_call" | custom-call | flops 44999999488 | bytes 12582912 | tf_op jit(solution)/shard_map/attn_dq/pallas_call | solution.py:1512
  202.6 18.7 %collective-permute-done.2.got_b = bf16[2,4,96,512]{3,2,1,0:T(8,128)(2,1)S(1)} collective-permute-done((bf16[2,4,96,512]{3,2,1,0:T(8,128)(2,1)}, bf16[2,4,96,512]{3,2,1,0:T(8,128)(2,1)S(1)}, u32[]{:S(2)}, u32[]{:S(2)}) %collective-permute-start.2) | collective-permute-done | bytes 786464 | tf_op jit(solution)/shard_map/ppermute | solution.py:1677
  221.3 0.0 copy-start.2
  221.3 6.6 %collective-permute-done.1.got_a = bf16[8,96,1216]{2,1,0:T(8,128)(2,1)S(1)} collective-permute-done((bf16[8,96,1216]{2,1,0:T(8,128)(2,1)}, bf16[8,96,1216]{2,1,0:T(8,128)(2,1)S(1)}, u32[]{:S(2)}, u32[]{:S(2)}) %collective-permute-start.1) | collective-permute-done | bytes 1867808 | tf_op jit(solution)/shard_map/ppermute | solution.py:1676
  227.9 0.0 copy-start
  227.9 0.0 copy-done.2
  227.9 1.3 copy-done
  229.2 4.7 %pair_sum.1 = (bf16[4,96,1216]{2,1,0:T(8,128)(2,1)}, bf16[4,96,1216]{2,1,0:T(8,128)(2,1)}, bf16[4,96,512]{2,1,0:T(8,128)(2,1)}, bf16[4,96,512]{2,1,0:T(8,128)(2,1)}) custom-call(bf16[8,96,1216]{2,1,0:T(8,128)(2,1)} %get-tuple-element.79.ours_a, bf16[8,96,1216]{2,1,0:T(8,128)(2,1)} %copy-done, bf16[2,4,96,512]{3,2,1,0:T(8,128)(2,1)} %get-tuple-element.81.ours_b, ...), custom_call_target="tpu_custom_call" | custom-call | flops 933888 | bytes 11206656 | tf_op jit(solution)/shard_map/pair_sum/pallas_call | solution.py:1203
  233.8 1.8 collective-permute-start.6
  235.6 0.4 collective-permute-start.5
  236.0 0.0 collective-permute-done.4.do_parts_2_
  236.0 0.0 collective-permute-done.3.do_parts_1_
  236.0 29.2 %attn_dkv.1 = (bf16[2048,192]{1,0:T(8,128)(2,1)}, bf16[2048,192]{1,0:T(8,128)(2,1)}) custom-call(s32[17]{0:T(128)} %pad_add_fusion.meta, bf16[2048,384]{1,0:T(8,128)(2,1)} %get-tuple-element.84.own, bf16[2048,256]{1,0:T(8,128)(2,1)} %get-tuple-element.73.query.q_ref.q_parts_0_, bf16[4096,256]{1,0:T(8,128)(2,1)} %bitcast.28, bf16[2048,256]{1,0:T(8,128)(2,1)} %bitcast.24, ...), custom_call_target="tpu_custom_call" | custom-call | flops 60000002048 | bytes 12582912 | tf_op jit(solution)/shard_map/attn_dkv/pallas_call | solution.py:1621
  265.1 0.0 collective-permute-done.6.got_b
  265.2 0.0 copy-start.3
  265.2 0.0 collective-permute-done.5.got_a
  265.2 0.0 copy-start.1
  265.2 0.7 copy-done.3
  265.9 0.4 copy-done.1
  266.3 71.1 %tail.1 = (f32[512,768]{1,0:T(8,128)}, f32[96,192]{1,0:T(8,128)}, f32[96,192]{1,0:T(8,128)}, f32[96,96]{1,0:T(8,128)}, f32[512,384]{1,0:T(8,128)}, /*index=5*/f3...) custom-call(bf16[2048,192]{1,0:T(8,128)(2,1)} %attn_dq.1.d_q, ...), custom_call_target="tpu_custom_call" | custom-call | tf_op jit(solution)/shard_map/tail/pallas_call | solution.py:463
  337.4 4.2 %settle.1 = (bf16[512,768]{1,0:T(8,128)(2,1)}, f32[512,768]{1,0:T(8,128)}, f32[96,192]{1,0:T(8,128)}, f32[96,192]{1,0:T(8,128)}, f32[96,96]{1,0:T(8,128)}, /*ind...) custom-call(bf16[512,768]{1,0:T(8,128)(2,1)} %get-tuple-element.74.r, ...), custom_call_target="tpu_custom_call" | custom-call | tf_op jit(solution)/shard_map/settle/pallas_call | solution.py:524
Async XLA Ops:
  0.6 92.5 %copy-start.5 = (s32[16]{0:T(128)S(1)}, s32[16]{0:T(128)}, u32[]{:S(2)}) copy-start(s32[16]{0:T(128)} %param.23) | copy-start | bytes 196
  90.0 25.7 %collective-permute-start = (bf16[3,96,1728]{2,1,0:T(8,128)(2,1)S(1)}, bf16[3,96,1728]{2,1,0:T(8,128)(2,1)S(1)}, u32[]{:S(2)}, u32[]{:S(2)}) collective-permute-start(bf16[3,96,1728]{2,1,0:T(8,128)(2,1)S(1)} %dynamic-slice_bitcast_fusion), channel_id=1, source_target_pairs={{0,16},{8,24},{16,0},{24,8},{1,17},{9,25},{17,1},{25,9},{2,18},{10... | collective-permute-start | bytes 2985992 | tf_op jit(solution)/shard_map/ppermute | solution.py:1666
  115.7 1.0 copy-start.4
  176.0 60.0 %collective-permute-start.4 = (bf16[2048,256]{1,0:T(8,128)(2,1)}, bf16[2048,256]{1,0:T(8,128)(2,1)}, u32[]{:S(2)}, u32[]{:S(2)}) collective-permute-start(bf16[2048,256]{1,0:T(8,128)(2,1)} %bitcast.21), channel_id=1, source_target_pairs={{2,0},{3,1},{4,2},{5,3},{6,4},{7,5},{10,8},{11,9},{12,10},{13,11},... | collective-permute-start | bytes 3145736 | tf_op jit(solution)/shard_map/ppermute | solution.py:1680
  177.3 58.7 %collective-permute-start.3 = (bf16[2048,256]{1,0:T(8,128)(2,1)}, bf16[2048,256]{1,0:T(8,128)(2,1)}, u32[]{:S(2)}, u32[]{:S(2)}) collective-permute-start(bf16[2048,256]{1,0:T(8,128)(2,1)} %bitcast.22), channel_id=1, source_target_pairs={{1,0},{2,1},{3,2},{4,3},{5,4},{6,5},{7,6},{9,8},{10,9},{11,10},{12... | collective-permute-start | bytes 3145736 | tf_op jit(solution)/shard_map/ppermute | solution.py:1680
  178.6 42.7 %collective-permute-start.2 = (bf16[2,4,96,512]{3,2,1,0:T(8,128)(2,1)}, bf16[2,4,96,512]{3,2,1,0:T(8,128)(2,1)S(1)}, u32[]{:S(2)}, u32[]{:S(2)}) collective-permute-start(bf16[2,4,96,512]{3,2,1,0:T(8,128)(2,1)} %get-tuple-element.76), channel_id=1, source_target_pairs={{0,1},{1,0},{2,3},{3,2},{4,5},{5,4},{6,7},{7,6},{8,9},{9,8},{10,11... | collective-permute-start | bytes 2359304 | tf_op jit(solution)/shard_map/ppermute | solution.py:1677
  181.3 46.6 %collective-permute-start.1 = (bf16[8,96,1216]{2,1,0:T(8,128)(2,1)}, bf16[8,96,1216]{2,1,0:T(8,128)(2,1)S(1)}, u32[]{:S(2)}, u32[]{:S(2)}) collective-permute-start(bf16[8,96,1216]{2,1,0:T(8,128)(2,1)} %get-tuple-element.75), channel_id=1, source_target_pairs={{0,16},{8,24},{16,0},{24,8},{1,17},{9,25},{17,1},{25,9},{2,18},{10... | collective-permute-start | bytes 5603336 | tf_op jit(solution)/shard_map/ppermute | solution.py:1676
  221.3 6.6 %copy-start.2 = (bf16[2,4,96,512]{3,2,1,0:T(8,128)(2,1)}, bf16[2,4,96,512]{3,2,1,0:T(8,128)(2,1)S(1)}, u32[]{:S(2)}) copy-start(bf16[2,4,96,512]{3,2,1,0:T(8,128)(2,1)S(1)} %collective-permute-done.2.got_b) | copy-start | bytes 2359300
  227.9 1.3 copy-start
  233.8 31.3 %collective-permute-start.6 = (bf16[4,96,512]{2,1,0:T(8,128)(2,1)}, bf16[4,96,512]{2,1,0:T(8,128)(2,1)S(1)}, u32[]{:S(2)}, u32[]{:S(2)}) collective-permute-start(bf16[4,96,512]{2,1,0:T(8,128)(2,1)} %get-tuple-element.95), channel_id=1, source_target_pairs={{0,16},{8,24},{16,0},{24,8},{1,17},{9,25},{17,1},{25,9},{2,18},{10... | collective-permute-start | bytes 1179656 | tf_op jit(solution)/shard_map/ppermute | solution.py:1689
  235.6 29.6 %collective-permute-start.5 = (bf16[4,96,1216]{2,1,0:T(8,128)(2,1)}, bf16[4,96,1216]{2,1,0:T(8,128)(2,1)S(1)}, u32[]{:S(2)}, u32[]{:S(2)}) collective-permute-start(bf16[4,96,1216]{2,1,0:T(8,128)(2,1)} %get-tuple-element.93), channel_id=1, source_target_pairs={{0,1},{1,0},{2,3},{3,2},{4,5},{5,4},{6,7},{7,6},{8,9},{9,8},{10,11... | collective-permute-start | bytes 2801672 | tf_op jit(solution)/shard_map/ppermute | solution.py:1688
  265.2 0.7 copy-start.3
  265.2 1.1 copy-start.1

commit v4 on v3

--- a/solution.py
+++ b/solution.py
@@ -1186,29 +1186,34 @@
 
 def pair_sum_kernel(ours_a, got_a, ours_b, got_b, keep_a, give_a, keep_b, give_b):
     odd = lax.rem(lax.axis_index("blk"), 2)
-    sums = [(ours_a[n].astype(F32) + got_a[n].astype(F32)).astype(BF16) for n in range(2)]
-    keep_a[0] = jnp.where(odd == 0, sums[0], sums[1])
-    give_a[0] = jnp.where(odd == 0, sums[1], sums[0])
-    give_b[0] = (ours_b[0, 0].astype(F32) + got_b[0, 0].astype(F32)).astype(BF16)
-    keep_b[0] = (ours_b[1, 0].astype(F32) + got_b[1, 0].astype(F32)).astype(BF16)
-
-
-def pair_sum(ours_a, got_a, ours_b, got_b):
+    for j in range(keep_a.shape[0]):
+        sums = [
+            (ours_a[2 * j + n].astype(F32) + got_a[2 * j + n].astype(F32)).astype(BF16)
+            for n in range(2)
+        ]
+        keep_a[j] = jnp.where(odd == 0, sums[0], sums[1])
+        give_a[j] = jnp.where(odd == 0, sums[1], sums[0])
+        give_b[j] = (ours_b[0, j].astype(F32) + got_b[0, j].astype(F32)).astype(BF16)
+        keep_b[j] = (ours_b[1, j].astype(F32) + got_b[1, j].astype(F32)).astype(BF16)
+
+
+def pair_sum(ours_a, got_a, ours_b, got_b, step=2):
     nblk, part, width = ours_a.shape
     other = ours_b.shape[3]
-    a_in = pl.BlockSpec((2, part, width), lambda i: (i, 0, 0))
-    b_in = pl.BlockSpec((2, 1, part, other), lambda i: (0, i, 0, 0))
-    out = lambda cols: pl.BlockSpec((1, part, cols), lambda i: (i, 0, 0))
+    a_in = pl.BlockSpec((2 * step, part, width), lambda i: (i, 0, 0))
+    b_in = pl.BlockSpec((2, step, part, other), lambda i: (0, i, 0, 0))
+    out = lambda cols: pl.BlockSpec((step, part, cols), lambda i: (i, 0, 0))
     shape = lambda cols: jax.ShapeDtypeStruct((nblk // 2, part, cols), BF16)
     return pl.pallas_call(
         pair_sum_kernel,
-        grid=(nblk // 2,),
+        grid=(nblk // 2 // step,),
         in_specs=[a_in, a_in, b_in, b_in],
         out_specs=[out(width)] * 2 + [out(other)] * 2,
         out_shape=[shape(width)] * 2 + [shape(other)] * 2,
         cost_estimate=pl.CostEstimate(
             flops=nblk * part * width, bytes_accessed=12 * nblk * part * width, transcendentals=0
         ),
+        compiler_params=pltpu.CompilerParams(vmem_limit_bytes=32 << 20),
         name="pair_sum",
     )(ours_a, got_a, ours_b, got_b)
 

time: 346 us -> 337 us (0.974)
  Pallas kernels: 289 us -> 283 us
  waiting for transfers between devices: 32.4 us -> 28.5 us
    pallas_call x1, Pallas kernels: 71.1 us -> 63.2 us  [tail(): pl.pallas_call(functools.partial(tail_kernel, nblk, pieces, cols), out_sh...]
    pallas_call x1, Pallas kernels: 4.66 us -> 0.93 us  [pair_sum(): pl.pallas_call(pair_sum_kernel, grid=(nblk // 2 // step,), in_specs=[a_in...]
  transfers between devices with their start and end apart: 7 -> 7, of which waited for: 3 -> 3; matrix products, arithmetic and copies ran while one was open for 0% -> 0% of each run, Pallas kernels for 20% -> 21%
where the time goes in v4:
time: 337 us; the launch traced here: 332 us
  Pallas kernels  283 us (84%)
  waiting for transfers between devices  28.5 us (8%)
  starting transfers between devices  13 us (4%)
  local copies, waits for them, and re-layouts  6.05 us (2%)
    pallas_call x1, Pallas kernels, front(): pl.pallas_call(functools.partial(front_kernel, nblk, parts, pieces, early...  88 us
    pallas_call x1, Pallas kernels, tail(): pl.pallas_call(functools.partial(tail_kernel, nblk, pieces, cols), out_sh...  63.2 us
    pallas_call x1, Pallas kernels, middle(): pl.pallas_call(functools.partial(middle_kernel, nblk, up_cols, cut, piece...  58 us
    pallas_call x1, Pallas kernels, attention_dkv(): pl.pallas_call(functools.partial(dkv_kernel, heads, ndocs, tq, tk), grid=...  31.6 us
    pallas_call x1, Pallas kernels, attention_dq(): pl.pallas_call(functools.partial(dq_kernel, heads, ndocs, tq, tk), grid=(...  20.6 us
    ppermute x1, waiting for transfers between devices, on_device(): got_b = lax.ppermute(give_b, 'blk', across)  17.2 us
    pallas_call x1, Pallas kernels, attention_fwd(): pl.pallas_call(functools.partial(fwd_kernel, heads, ndocs, tq, tk), grid=...  16.6 us
  transfers between devices with their start and end apart: 7, of which 3 were waited for; matrix products, arithmetic and copies ran while one was open for 0% of the time, Pallas kernels for 21%

profile of v4, /device:TPU:0, one launch (start us, length us, event | category | flops | bytes accessed | tf_op | source)
XLA Modules:
  0.0 332.3 jit_solution(5958626426274671066)
XLA Ops:
  0.6 0.0 copy-start.8
  0.7 88.0 %front.1 = (bf16[2048,768]{1,0:T(8,128)(2,1)}, bf16[2048,256]{1,0:T(8,128)(2,1)}, bf16[2048,384]{1,0:T(8,128)(2,1)}, bf16[2,2048,384]{2,1,0:T(8,128)(2,1)}, bf16...) custom-call(bf16[512,768]{1,0:T(8,128)(2,1)} %tok.5, ...), custom_call_target="tpu_custom_call" | custom-call | tf_op jit(solution)/shard_map/front/pallas_call | solution.py:834
  88.7 1.3 dynamic-slice_bitcast_fusion
  90.0 3.1 collective-permute-start
  93.1 0.0 copy-done.8
  93.1 0.6 pad_add_fusion.meta
  93.7 16.6 %attn_fwd.1 = (bf16[4,512,192]{2,1,0:T(8,128)(2,1)}, bf16[2048,256]{1,0:T(8,128)(2,1)}) custom-call(s32[17]{0:T(128)} %pad_add_fusion.meta, bf16[2048,256]{1,0:T(8,128)(2,1)} %get-tuple-element.66.q_ref, bf16[4096,384]{1,0:T(8,128)(2,1)} %bitcast.19, bf16[2048,384]{1,0:T(8,128)(2,1)} %get-tuple-element.84.own), custom_call_target="tpu_custom_call" | custom-call | flops 30000001024 | bytes 12582912 | tf_op jit(solution)/shard_map/attn_fwd/pallas_call | solution.py:1439
  110.3 5.4 %collective-permute-done.late = bf16[3,96,1728]{2,1,0:T(8,128)(2,1)S(1)} collective-permute-done((bf16[3,96,1728]{2,1,0:T(8,128)(2,1)S(1)}, bf16[3,96,1728]{2,1,0:T(8,128)(2,1)S(1)}, u32[]{:S(2)}, u32[]{:S(2)}) %collective-permute-start) | collective-permute-done | bytes 995360 | tf_op jit(solution)/shard_map/ppermute | solution.py:1671
  115.7 0.0 copy-start.7
  115.7 1.0 copy-done.7
  116.7 58.0 %middle.1 = (bf16[512,768]{1,0:T(8,128)(2,1)}, f32[512,768]{1,0:T(8,128)}, bf16[4,512,256]{2,1,0:T(8,128)(2,1)}, f32[1,768]{1,0:T(1,128)}, bf16[8,96,1216]{2,1,0...) custom-call(bf16[512,768]{1,0:T(8,128)(2,1)} %tok.5, ...), custom_call_target="tpu_custom_call" | custom-call | flops 16307453952 | bytes 25165824 | tf_op jit(solution)/shard_map/middle/pallas_call | solution.py:1146
  174.7 1.3 collective-permute-start.4
  176.0 1.3 collective-permute-start.3
  177.3 2.7 collective-permute-start.2
  180.0 0.0 copy-start
  180.0 0.0 copy-start.2
  180.0 2.5 collective-permute-start.1
  182.5 20.6 %attn_dq.1.d_q = bf16[2048,192]{1,0:T(8,128)(2,1)} custom-call(s32[17]{0:T(128)} %pad_add_fusion.meta, bf16[2048,256]{1,0:T(8,128)(2,1)} %get-tuple-element.73.query.q_ref.q_parts_0_, bf16[2048,256]{1,0:T(8,128)(2,1)} %bitcast.23, bf16[4096,384]{1,0:T(8,128)(2,1)} %bitcast.20, bf16[2048,384]{1,0:T(8,128)(2,1)} %get-tuple-element.84.own), custom_call_target="tpu_custom_call" | custom-call | flops 44999999488 | bytes 12582912 | tf_op jit(solution)/shard_map/attn_dq/pallas_call | solution.py:1517
  203.2 17.2 %collective-permute-done.2.got_b = bf16[2,4,96,512]{3,2,1,0:T(8,128)(2,1)S(1)} collective-permute-done((bf16[2,4,96,512]{3,2,1,0:T(8,128)(2,1)}, bf16[2,4,96,512]{3,2,1,0:T(8,128)(2,1)S(1)}, u32[]{:S(2)}, u32[]{:S(2)}) %collective-permute-start.2) | collective-permute-done | bytes 786464 | tf_op jit(solution)/shard_map/ppermute | solution.py:1682
  220.4 5.9 %collective-permute-done.1.got_a = bf16[8,96,1216]{2,1,0:T(8,128)(2,1)S(1)} collective-permute-done((bf16[8,96,1216]{2,1,0:T(8,128)(2,1)}, bf16[8,96,1216]{2,1,0:T(8,128)(2,1)S(1)}, u32[]{:S(2)}, u32[]{:S(2)}) %collective-permute-start.1) | collective-permute-done | bytes 1867808 | tf_op jit(solution)/shard_map/ppermute | solution.py:1681
  226.3 0.0 copy-done
  226.3 0.0 copy-done.2
  226.3 0.9 pair_sum.1
  227.2 0.0 copy-start.1
  227.2 0.9 copy-done.1
  228.2 0.0 copy-start.3
  228.2 0.7 copy-done.3
  228.9 1.7 collective-permute-start.6
  230.7 0.4 collective-permute-start.5
  231.0 0.0 collective-permute-done.4.do_parts_2_
  231.1 0.0 copy-start.6
  231.1 0.0 collective-permute-done.3.do_parts_1_
  231.1 1.0 copy-done.6
  232.0 31.6 %attn_dkv.1 = (bf16[2048,192]{1,0:T(8,128)(2,1)}, bf16[2048,192]{1,0:T(8,128)(2,1)}) custom-call(s32[17]{0:T(128)} %pad_add_fusion.meta, bf16[2048,384]{1,0:T(8,128)(2,1)} %get-tuple-element.84.own, bf16[2048,256]{1,0:T(8,128)(2,1)} %get-tuple-element.73.query.q_ref.q_parts_0_, bf16[4096,256]{1,0:T(8,128)(2,1)} %bitcast.28, bf16[2048,256]{1,0:T(8,128)(2,1)} %bitcast.24, ...), custom_call_target="tpu_custom_call" | custom-call | flops 60000002048 | bytes 12582912 | tf_op jit(solution)/shard_map/attn_dkv/pallas_call | solution.py:1626
  263.6 0.0 collective-permute-done.6.got_b
  263.6 0.0 copy-start.5
  263.6 0.0 collective-permute-done.5.got_a
  263.6 0.0 copy-start.4
  263.6 0.7 copy-done.5
  264.3 0.4 copy-done.4
  264.7 63.2 %tail.1 = (f32[512,768]{1,0:T(8,128)}, f32[96,192]{1,0:T(8,128)}, f32[96,192]{1,0:T(8,128)}, f32[96,96]{1,0:T(8,128)}, f32[512,384]{1,0:T(8,128)}, /*index=5*/f3...) custom-call(bf16[2048,192]{1,0:T(8,128)(2,1)} %attn_dq.1.d_q, ...), custom_call_target="tpu_custom_call" | custom-call | tf_op jit(solution)/shard_map/tail/pallas_call | solution.py:463
  327.9 4.2 %settle.1 = (bf16[512,768]{1,0:T(8,128)(2,1)}, f32[512,768]{1,0:T(8,128)}, f32[96,192]{1,0:T(8,128)}, f32[96,192]{1,0:T(8,128)}, f32[96,96]{1,0:T(8,128)}, /*ind...) custom-call(bf16[512,768]{1,0:T(8,128)(2,1)} %get-tuple-element.74.r, ...), custom_call_target="tpu_custom_call" | custom-call | tf_op jit(solution)/shard_map/settle/pallas_call | solution.py:524
Async XLA Ops:
  0.6 92.5 %copy-start.8 = (s32[16]{0:T(128)S(1)}, s32[16]{0:T(128)}, u32[]{:S(2)}) copy-start(s32[16]{0:T(128)} %param.23) | copy-start | bytes 196
  90.0 25.7 %collective-permute-start = (bf16[3,96,1728]{2,1,0:T(8,128)(2,1)S(1)}, bf16[3,96,1728]{2,1,0:T(8,128)(2,1)S(1)}, u32[]{:S(2)}, u32[]{:S(2)}) collective-permute-start(bf16[3,96,1728]{2,1,0:T(8,128)(2,1)S(1)} %dynamic-slice_bitcast_fusion), channel_id=1, source_target_pairs={{0,16},{8,24},{16,0},{24,8},{1,17},{9,25},{17,1},{25,9},{2,18},{10... | collective-permute-start | bytes 2985992 | tf_op jit(solution)/shard_map/ppermute | solution.py:1671
  115.7 1.0 copy-start.7
  174.7 56.3 %collective-permute-start.4 = (bf16[2048,256]{1,0:T(8,128)(2,1)}, bf16[2048,256]{1,0:T(8,128)(2,1)S(1)}, u32[]{:S(2)}, u32[]{:S(2)}) collective-permute-start(bf16[2048,256]{1,0:T(8,128)(2,1)} %bitcast.21), channel_id=1, source_target_pairs={{2,0},{3,1},{4,2},{5,3},{6,4},{7,5},{10,8},{11,9},{12,10},{13,11},... | collective-permute-start | bytes 3145736 | tf_op jit(solution)/shard_map/ppermute | solution.py:1685
  176.0 55.0 %collective-permute-start.3 = (bf16[2048,256]{1,0:T(8,128)(2,1)}, bf16[2048,256]{1,0:T(8,128)(2,1)}, u32[]{:S(2)}, u32[]{:S(2)}) collective-permute-start(bf16[2048,256]{1,0:T(8,128)(2,1)} %bitcast.22), channel_id=1, source_target_pairs={{1,0},{2,1},{3,2},{4,3},{5,4},{6,5},{7,6},{9,8},{10,9},{11,10},{12... | collective-permute-start | bytes 3145736 | tf_op jit(solution)/shard_map/ppermute | solution.py:1685
  177.3 43.1 %collective-permute-start.2 = (bf16[2,4,96,512]{3,2,1,0:T(8,128)(2,1)}, bf16[2,4,96,512]{3,2,1,0:T(8,128)(2,1)S(1)}, u32[]{:S(2)}, u32[]{:S(2)}) collective-permute-start(bf16[2,4,96,512]{3,2,1,0:T(8,128)(2,1)} %get-tuple-element.76), channel_id=1, source_target_pairs={{0,1},{1,0},{2,3},{3,2},{4,5},{5,4},{6,7},{7,6},{8,9},{9,8},{10,11... | collective-permute-start | bytes 2359304 | tf_op jit(solution)/shard_map/ppermute | solution.py:1682
  180.0 46.3 %copy-start = (bf16[8,96,1216]{2,1,0:T(8,128)(2,1)S(1)}, bf16[8,96,1216]{2,1,0:T(8,128)(2,1)}, u32[]{:S(2)}) copy-start(bf16[8,96,1216]{2,1,0:T(8,128)(2,1)} %get-tuple-element.79.ours_a) | copy-start | bytes 5603332
  180.0 46.3 %copy-start.2 = (bf16[2,4,96,512]{3,2,1,0:T(8,128)(2,1)S(1)}, bf16[2,4,96,512]{3,2,1,0:T(8,128)(2,1)}, u32[]{:S(2)}) copy-start(bf16[2,4,96,512]{3,2,1,0:T(8,128)(2,1)} %get-tuple-element.81.ours_b) | copy-start | bytes 2359300
  180.0 46.3 %collective-permute-start.1 = (bf16[8,96,1216]{2,1,0:T(8,128)(2,1)}, bf16[8,96,1216]{2,1,0:T(8,128)(2,1)S(1)}, u32[]{:S(2)}, u32[]{:S(2)}) collective-permute-start(bf16[8,96,1216]{2,1,0:T(8,128)(2,1)} %get-tuple-element.75), channel_id=1, source_target_pairs={{0,16},{8,24},{16,0},{24,8},{1,17},{9,25},{17,1},{25,9},{2,18},{10... | collective-permute-start | bytes 5603336 | tf_op jit(solution)/shard_map/ppermute | solution.py:1681
  227.2 0.9 copy-start.1
  228.2 0.7 copy-start.3
  228.9 34.7 %collective-permute-start.6 = (bf16[4,96,512]{2,1,0:T(8,128)(2,1)S(1)}, bf16[4,96,512]{2,1,0:T(8,128)(2,1)S(1)}, u32[]{:S(2)}, u32[]{:S(2)}) collective-permute-start(bf16[4,96,512]{2,1,0:T(8,128)(2,1)S(1)} %get-tuple-element.95), channel_id=1, source_target_pairs={{0,16},{8,24},{16,0},{24,8},{1,17},{9,25},{17,1},{25,9},{2,18},{10... | collective-permute-start | bytes 1179656 | tf_op jit(solution)/shard_map/ppermute | solution.py:1694
  230.7 32.9 %collective-permute-start.5 = (bf16[4,96,1216]{2,1,0:T(8,128)(2,1)S(1)}, bf16[4,96,1216]{2,1,0:T(8,128)(2,1)S(1)}, u32[]{:S(2)}, u32[]{:S(2)}) collective-permute-start(bf16[4,96,1216]{2,1,0:T(8,128)(2,1)S(1)} %get-tuple-element.93), channel_id=1, source_target_pairs={{0,1},{1,0},{2,3},{3,2},{4,5},{5,4},{6,7},{7,6},{8,9},{9,8},{10,11... | collective-permute-start | bytes 2801672 | tf_op jit(solution)/shard_map/ppermute | solution.py:1693
  231.1 1.0 copy-start.6
  263.6 0.7 copy-start.5
  263.6 1.1 copy-start.4
